TPU v7x, 32 devices: a whole 2x2x4 slice. The times are simulated.
32 devices in a mesh: dp: 4 (over x, core), row: 2 (over y), col: 4 (over z).
Axes of the slice: x: 2, y: 2, z: 4, core: 2. Of those that a mesh axis runs over, the one named last changes fastest.
Arguments:
- hidden_in: bfloat16 [4096, 2048], P(('dp', 'col'), 'row'), may hold values from -6 to 6
- segment: int32 [4, 1024], P('dp'), may hold values from 0 to 3, never falling along the last dimension, each value on 1 to 512 neighbouring positions
- norm1_gain: float32 [2048], P('row'), may hold values from 0.5 to 1.5
- norm1_bias: float32 [2048], P('row'), may hold values from -2 to 2
- norm2_gain: float32 [2048], P('row'), may hold values from 0.5 to 1.5
- norm2_bias: float32 [2048], P('row'), may hold values from -2 to 2
- qkv_weight: bfloat16 [2048, 6144], P('row', 'col'), may hold values from -1 to 1
- qkv_bias: float32 [6144], P('col'), may hold values from -2 to 2
- dense_weight: bfloat16 [2048, 2048], P('col', 'row'), may hold values from -1 to 1
- dense_bias: float32 [2048], P('row'), may hold values from -2 to 2
- up_weight: bfloat16 [2048, 8192], P('row', 'col'), may hold values from -0.125 to 0.125
- up_bias: float32 [8192], P('col'), may hold values from -3 to 3
- down_weight: bfloat16 [8192, 2048], P('col', 'row'), may hold values from -0.0625 to 0.0625
- down_bias: float32 [2048], P('row'), may hold values from -2 to 2
- cotangent: bfloat16 [4096, 2048], P(('dp', 'col'), 'row'), may hold values from -6 to 6
Outputs:
- block_out: bfloat16 [4096, 2048], P(('dp', 'col'), 'row')
- input_grad: float32 [4096, 2048], P(('dp', 'col'), 'row')
- norm1_gain_grad: float32 [2048], P('row')
- norm1_bias_grad: float32 [2048], P('row')
- norm2_gain_grad: float32 [2048], P('row')
- norm2_bias_grad: float32 [2048], P('row')
- qkv_weight_grad: float32 [2048, 6144], P('row', 'col')
- qkv_bias_grad: float32 [6144], P('col')
- dense_weight_grad: float32 [2048, 2048], P('col', 'row')
- dense_bias_grad: float32 [2048], P('row')
- up_weight_grad: float32 [2048, 8192], P('row', 'col')
- up_bias_grad: float32 [8192], P('col')
- down_weight_grad: float32 [8192, 2048], P('col', 'row')
- down_bias_grad: float32 [2048], P('row')
Inputs may be any that keep to these rules, and one draw needn't show every extreme that they name: Each row holds one data group's 1024 token slots; segment numbers never fall along a row, a run of equal numbers is one sequence of at most 512 tokens, and some sequence is exactly 512 long.
All inputs are finite; a program needn't handle non-finite values.
Results may differ from a plain program's by a relative error of at most 0.0093.
Values may be sent and summed in bfloat16 or wider, within the bound.
A program may use at most 192 MiB of HBM per device.

v0:
```python
import functools
import math

import jax
import jax.numpy as jnp
from jax import lax
from jax.experimental import pallas as pl
from jax.experimental.pallas import tpu as pltpu
from jax.sharding import PartitionSpec as P

HD = 256
ROT = 64
F32 = jnp.float32
BF16 = jnp.bfloat16
MESH = pl.DeviceIdType.MESH

eps_norm = 1e-05
rope_base = 10000.0
TILE = 512
NN = (((1,), (0,)), ((), ()))
NT = (((1,), (1,)), ((), ()))
TN = (((0,), (0,)), ((), ()))


def dot(left, right, dims):
    return lax.dot_general(left, right, dims, preferred_element_type=F32)


class Copies:
    def __init__(self, send_sem, recv_sem):
        self.send_sem, self.recv_sem = send_sem, recv_sem
        self.made, self.open = {}, {}

    def start(self, name, source, target, device, when=None):
        index = len(self.made)
        copy = pltpu.make_async_remote_copy(
            src_ref=source,
            dst_ref=target,
            send_sem=self.send_sem.at[index],
            recv_sem=self.recv_sem.at[index],
            device_id=device,
            device_id_type=MESH,
        )
        self.made[name] = copy
        self.open[name] = when
        guarded(when, copy.start)

    def came(self, name, when=None):
        guarded(when, self.made[name].wait_recv)

    def sent(self, *names):
        for name in names:
            guarded(self.open.pop(name), self.made[name].wait_send)

    def sent_all(self):
        self.sent(*list(self.open))


def guarded(when, action):
    if when is None:
        action()
    else:
        pl.when(when)(action)


def at(start, size):
    return pl.ds(pl.multiple_of(start, size), size)


def tiles(count, body):
    lax.fori_loop(0, count, lambda i, carry: (body(i), carry)[1], 0)


def step_kernel(
    sizes,
    hid, cot, wq, wu, wd, wn, seg, gain1, bias1, gain2, bias2, qkv_b, up_b, dense_b, down_b,
    out, in_grad, small, g_qkv, g_dense, g_up, g_down,
    X, G, WQ, WU, WD, WN, N, STAT, QKV, ATT, HID, SLOPE, DUP, DAT, OUTP, ORECV, OY, DZ,
    S_dn, S_de, S_up, S_qk, R_dn, R_de, X_dn, X_de, A_de, TMP, NV, COS, SIN, NSUM, SM, SMO, SMR,
    send_sem, recv_sem, local_sem, credit,
):
    blk, wid, cols = sizes
    rows_all = blk * cols
    width = 2 * wid
    heads, units = WQ.shape[1], WU.shape[1]
    hh, uh, dh = heads // 2, units // 2, HD // 2
    r = lax.axis_index("row")
    c = lax.axis_index("col")
    dp = lax.axis_index("dp")
    k = lax.rem(dp, 2)
    hi = lax.rem(lax.div(dp, 2), 2)
    q = k + 2 * hi
    core_dev = {"dp": dp + 1 - 2 * k}
    x_dev = {"dp": dp + 2 - 4 * hi}
    y_dev = {"row": 1 - r}
    c_low, c_high = lax.rem(c, 2), lax.div(c, 2)
    col_of = [c, c + 1 - 2 * c_low, c + 2 - 4 * c_high, 3 - c]
    own, other = pl.ds(0, wid), pl.ds(wid, wid)
    scale = 1.0 / math.sqrt(HD)
    copies = Copies(send_sem, recv_sem)

    barrier = pltpu.get_barrier_semaphore()
    friends = [core_dev, x_dev, y_dev] + [{"col": col_of[s]} for s in (1, 2, 3)]
    for device in friends:
        pl.semaphore_signal(barrier, inc=1, device_id=device, device_id_type=MESH)

    local = []

    def fetch(source, target):
        copy = pltpu.make_async_copy(source, target, local_sem.at[len(local)])
        copy.start()
        local.append(copy)
        return copy

    fetch_x = fetch(hid, X.at[at(c * blk, blk), own])
    fetch_g = fetch(cot, G.at[at(c * blk, blk), own])
    fetch_u = fetch(wu.at[:, at(r * units, units)], WU.at[own, :])
    fetch_q = fetch(wq.at[:, at(r * heads, heads)], WQ.at[own, :])
    fetch_n = fetch(wn.at[at(r * units, units), :], WN.at[:, own])
    fetch_d = fetch(wd.at[at(r * HD, HD), :], WD.at[:, own])
    pl.semaphore_wait(barrier, len(friends))

    def rows(b):
        return at(b * blk, blk)

    def chain_send(tag, step, buf, columns, first=None):
        for word, move, edge in (("u", 1, c < cols - 1), ("d", -1, c >= 1)):
            block = c - move * (step - 1)
            valid = edge & (block >= 0) & (block <= cols - 1)
            source = first if first is not None else buf.at[rows(block), columns]
            copies.start(
                f"{tag}{word}{step}", source, buf.at[rows(block), columns], {"col": c + move}, valid
            )

    def chain_wait(tag, step):
        copies.came(f"{tag}u{step}", c >= step)
        copies.came(f"{tag}d{step}", c + step <= cols - 1)

    def row_send(name, s):
        b = col_of[s]
        copies.start(name, X.at[rows(b), own], X.at[rows(b), other], y_dev)

    q2 = q + 2 - 4 * hi

    def weight(name, source, full, row0, size, columns):
        def place(quarter):
            return full.at[at(row0 + quarter * size, size), columns]

        copies.start(f"{name}y", source, place(q), y_dev)

        def pass_on():
            copies.came(f"{name}y")
            copies.start(f"{name}x", place(q), place(q), x_dev)
            copies.start(f"{name}c", place(q), place(q), core_dev)

        def pass_far():
            copies.came(f"{name}x")
            copies.start(f"{name}f", place(q2), place(q2), core_dev)

        def done():
            copies.came(f"{name}c")
            copies.came(f"{name}f")

        return pass_on, pass_far, done

    everything = slice(None)
    chain_send("x", 1, X, own, hid)
    copies.start("xy0", hid, X.at[rows(c), other], y_dev)
    for j, vector in enumerate((gain1, bias1, gain2, bias2)):
        copies.start(f"nv{j}", vector, NV.at[pl.ds(j, 1), other], y_dev)
    wq4, wn4, wd4 = wid // 4, units // 4, HD // 4
    wu_on, wu_far, wu_done = weight(
        "wu", wu.at[at(q * wq4, wq4), at((1 - r) * units, units)], WU, wid, wq4, everything
    )

    seg_row = seg[...].astype(F32)
    seg_col = jnp.transpose(jnp.broadcast_to(seg_row, (128, rows_all)))
    STAT[:, 3:4] = seg_col[:, 0:1]
    for j, vector in enumerate((gain1, bias1, gain2, bias2)):
        NV[j : j + 1, own] = vector[...]

    def table(i):
        block = at(i * blk, blk)
        starts = jnp.sum(
            (seg_row < STAT[block, 3:4]).astype(F32), axis=1, keepdims=True
        )
        index = lax.broadcasted_iota(jnp.int32, (blk, 1), 0) + i * blk
        lane = lax.broadcasted_iota(jnp.int32, (1, 128), 1)
        turn = jnp.exp(
            lax.rem(lane, ROT // 2).astype(F32) * (-2.0 * math.log(rope_base) / ROT)
        )
        angles = (index.astype(F32) - starts) * turn
        COS[block, :] = jnp.where(lane < ROT, jnp.cos(angles), 1.0)
        SIN[block, :] = jnp.where(
            lane < ROT // 2, -jnp.sin(angles), jnp.where(lane < ROT, jnp.sin(angles), 0.0)
        )

    tiles(cols, table)

    def rotate(head, block, sign):
        first = head[:, :128]
        lane = lax.broadcasted_iota(jnp.int32, first.shape, 1)
        swapped = jnp.where(
            lane < ROT // 2, pltpu.roll(first, 128 - ROT // 2, 1), pltpu.roll(first, ROT // 2, 1)
        )
        turned = first * COS[block, :] + sign * (swapped * SIN[block, :])
        return jnp.concatenate([turned, head[:, 128:]], axis=1)

    sub = 64

    def norm_block(b):
        def part(i):
            rs = at(b * blk + i * sub, sub)
            x = X[rs, :].astype(F32)
            mean = jnp.sum(x, axis=1, keepdims=True) * (1.0 / width)
            square = jnp.sum(x * x, axis=1, keepdims=True) * (1.0 / width)
            inv = lax.rsqrt(square - mean * mean + eps_norm)
            STAT[rs, 0:1] = mean
            STAT[rs, 1:2] = inv
            normal = (x - mean) * inv
            OUTP[rs, :] = (normal * NV[0:1, :] + NV[1:2, :]).astype(BF16)
            N[rs, :] = (normal * NV[2:3, :] + NV[3:4, :]).astype(BF16)

        tiles(blk // sub, part)

    def up_block(b):
        def part(j):
            cs = at(j * TILE, TILE)
            bias = up_b[:, at(r * units + j * TILE, TILE)]
            up = dot(N[rows(b), :], WU[:, cs], NN) + bias
            cdf = 0.5 * (1.0 + lax.erf(up * (1.0 / math.sqrt(2.0))))
            HID[rows(b), cs] = (up * cdf).astype(BF16)
            SLOPE[rows(b), cs] = (
                cdf + up * jnp.exp(-0.5 * up * up) * (1.0 / math.sqrt(2.0 * math.pi))
            ).astype(BF16)

        tiles(units // TILE, part)

    fetch_x.wait()
    fetch_g.wait()
    chain_wait("x", 1)
    chain_send("x", 2, X, own)
    row_send("xy1", 1)
    copies.start("gy", cot, G.at[rows(c), other], y_dev)
    wu_on()
    chain_wait("x", 2)
    chain_send("x", 3, X, own)
    row_send("xy2", 2)
    chain_send("g", 1, G, own, cot)
    wu_far()
    fetch_u.wait()
    for j in range(4):
        copies.came(f"nv{j}")
    copies.came("xy0")
    norm_block(col_of[0])
    chain_wait("x", 3)
    row_send("xy3", 3)
    wq_on, wq_far, wq_done = weight(
        "wq", wq.at[at(q * wq4, wq4), at((1 - r) * heads, heads)], WQ, wid, wq4, everything
    )
    wn_on, wn_far, wn_done = weight(
        "wn", wn.at[at((1 - r) * units + q * wn4, wn4), :], WN, 0, wn4, other
    )
    wd_on, wd_far, wd_done = weight(
        "wd", wd.at[at((1 - r) * HD + q * wd4, wd4), :], WD, 0, wd4, other
    )
    wu_done()
    up_block(col_of[0])
    copies.came("xy1")
    norm_block(col_of[1])
    up_block(col_of[1])
    chain_wait("g", 1)
    chain_send("g", 2, G, own)
    copies.came("xy2")
    norm_block(col_of[2])
    up_block(col_of[2])
    copies.came("xy3")
    norm_block(col_of[3])
    chain_wait("g", 2)
    chain_send("g", 3, G, own)
    copies.came("gy")
    chain_send("h", 1, G, other)
    up_block(col_of[3])

    def grad_send(name, staged, left, right, n_rows, n_cols, target):
        def part(i):
            cs = at(i * TILE, TILE)
            staged[:, cs] = dot(left(None), right(cs), TN).astype(BF16)

        tiles(n_cols // TILE, part)
        copies.start(name, staged, target, core_dev)

    hid_keep, hid_send = at(k * uh, uh), at((1 - k) * uh, uh)
    att_keep, att_send = at(k * dh, dh), at((1 - k) * dh, dh)

    def out_grad(name, side, left_ref, keep, give, staged, landing):
        base = side * wid

        def give_part(i):
            cs = at(i * TILE, TILE)
            staged[:, cs] = dot(
                left_ref[:, give], G[:, at(base + i * TILE, TILE)], TN
            ).astype(BF16)

        tiles(wid // TILE, give_part)
        copies.start(f"{name}a", staged, landing, core_dev)

    def out_keep(name, side, left_ref, keep, landing):
        base = side * wid
        copies.came(f"{name}a")

        def keep_part(i):
            cs = at(i * TILE, TILE)
            mine = dot(left_ref[:, keep], G[:, at(base + i * TILE, TILE)], TN)
            landing[:, cs] = (mine + landing[:, cs].astype(F32)).astype(BF16)

        tiles(wid // TILE, keep_part)

    chain_wait("g", 3)
    out_grad("dn0", 0, HID, hid_keep, hid_send, DUP.at[pl.ds(0, uh), :], S_dn.at[0])
    out_keep("dn0", 0, HID, hid_keep, S_dn.at[0])
    copies.start("dn0x", S_dn.at[0], X_dn.at[0], x_dev)

    wq_on()
    fetch_q.wait()
    chain_wait("h", 1)
    chain_send("h", 2, G, other)
    wn_on()
    wd_on()
    wq_far()
    wq_done()

    def qkv_block(i):
        block = at(i * blk, blk)
        for j in range(3):
            bias = qkv_b[:, at(r * heads + j * HD, HD)]
            value = dot(OUTP[block, :], WQ[:, j * HD : (j + 1) * HD], NN) + bias
            if j < 2:
                value = rotate(value, block, 1.0)
            QKV[block, j * HD : (j + 1) * HD] = value.astype(BF16)

    tiles(cols, qkv_block)
    wn_far()
    wd_far()

    def key_range(i):
        low = max(0, i - 2) * blk
        return slice(i * blk, (i + 1) * blk), slice(low, (i + 1) * blk), low

    def block_scores(i):
        mine, span, low = key_range(i)
        n = span.stop - low
        s = dot(QKV[mine, 0:HD], QKV[span, HD : 2 * HD], NT) * scale
        row_id = lax.broadcasted_iota(jnp.int32, (blk, n), 0) + i * blk
        col_id = lax.broadcasted_iota(jnp.int32, (blk, n), 1) + low
        same = STAT[mine, 3:4] == seg_row[:, span]
        return jnp.where(same & (col_id <= row_id), s, -1e30)

    for i in range(cols):
        mine, span, low = key_range(i)
        s = block_scores(i)
        largest = jnp.max(s, axis=1, keepdims=True)
        p = jnp.exp(s - largest)
        total = jnp.sum(p, axis=1, keepdims=True)
        STAT[mine, 2:3] = largest + jnp.log(total)
        p_low = (p / total).astype(BF16)
        ATT[mine, :] = dot(p_low, QKV[span, 2 * HD :], NN).astype(BF16)
    chain_wait("h", 2)
    chain_send("h", 3, G, other)
    fetch_n.wait()
    fetch_d.wait()
    wn_done()
    wd_done()

    def branch_block(b):
        def part(j):
            cs = at(j * TILE, TILE)
            both = dot(ATT[rows(b), :], WD[:, cs], NN) + dot(HID[rows(b), :], WN[:, cs], NN)
            OUTP[rows(b), cs] = both.astype(BF16)

        tiles(width // TILE, part)

    chain_wait("h", 3)
    for s in (1, 2, 3):
        branch_block(col_of[s])
        copies.start(
            f"oz{s}", OUTP.at[rows(col_of[s]), :], ORECV.at[s - 1], {"col": col_of[s]}
        )
    out_grad("dn1", 1, HID, hid_keep, hid_send, DUP.at[pl.ds(uh, uh), :], S_dn.at[1])
    out_grad("de0", 0, ATT, att_keep, att_send, A_de.at[0], S_de.at[0])
    out_grad("de1", 1, ATT, att_keep, att_send, A_de.at[1], S_de.at[1])
    out_keep("dn1", 1, HID, hid_keep, S_dn.at[1])
    copies.start("dn1y", S_dn.at[1], R_dn, y_dev)
    branch_block(col_of[0])

    copies.sent("dn0a", "dn1a")

    def up_grad_part(i):
        block = at(i * blk, blk)
        for j in range(units // TILE):
            cs = slice(j * TILE, (j + 1) * TILE)
            back = dot(G[block, :], WN[cs, :], NT)
            DUP[block, cs] = (back * SLOPE[block, cs].astype(F32)).astype(BF16)

    tiles(cols, up_grad_part)
    keep_u, give_u = at(k * uh, uh), at((1 - k) * uh, uh)
    keep_h, give_h = at(k * hh, hh), at((1 - k) * hh, hh)

    def in_give(name, right_ref, give, n, staged, landing):
        for side in (0, 1):

            def part(i):
                rs = at(i * TILE, TILE)
                lefts = N[:, at(side * wid + i * TILE, TILE)]
                staged[side][rs, :] = dot(lefts, right_ref[:, give], TN).astype(BF16)

            tiles(wid // TILE, part)
            copies.start(f"{name}{side}a", staged[side], landing.at[side], core_dev)

    def in_keep(name, side, right_ref, keep, landing):
        copies.came(f"{name}{side}a")

        def part(i):
            rs = at(i * TILE, TILE)
            mine = dot(N[:, at(side * wid + i * TILE, TILE)], right_ref[:, keep], TN)
            landing[side, rs, :] = (mine + landing[side, rs, :].astype(F32)).astype(BF16)

        tiles(wid // TILE, part)

    in_give(
        "up", DUP, give_u, uh, [HID.at[:, pl.ds(0, uh)], HID.at[:, pl.ds(uh, uh)]], S_up
    )
    for i in range(cols):
        mine = slice(i * blk, (i + 1) * blk)
        DAT[mine, :] = dot(G[mine, :], WD[...], NT).astype(BF16)
    SM[6:7, :] = jnp.sum(G[:, own].astype(F32), axis=0, keepdims=True)
    out_keep("de0", 0, ATT, att_keep, S_de.at[0])
    out_keep("de1", 1, ATT, att_keep, S_de.at[1])

    copies.sent(*[f"{t}{w}{s}" for t in "gh" for w in "ud" for s in (1, 2, 3)])
    copies.sent("wnx", "wnc", "wnf")
    pl.semaphore_signal(credit.at[0], inc=1, device_id=x_dev, device_id_type=MESH)
    pl.semaphore_signal(credit.at[1], inc=1, device_id=y_dev, device_id_type=MESH)
    R_up, X_up = G.at[:, pl.ds(2 * uh, uh)], [G.at[:, pl.ds(j * uh, uh)] for j in (0, 1)]
    R_qk, X_qk = WN.at[:, pl.ds(2 * hh, hh)], [WN.at[:, pl.ds(j * hh, hh)] for j in (0, 1)]

    in_keep("up", 0, DUP, keep_u, S_up)
    pl.semaphore_wait(credit.at[0], 1)
    copies.start("up0x", S_up.at[0], X_up[0], x_dev)
    in_keep("up", 1, DUP, keep_u, S_up)
    pl.semaphore_wait(credit.at[1], 1)
    copies.start("up1y", S_up.at[1], R_up, y_dev)
    copies.start("de0x", S_de.at[0], X_de.at[0], x_dev)
    copies.start("de1y", S_de.at[1], R_de, y_dev)
    copies.sent("up0a", "up1a")
    pl.semaphore_signal(credit.at[2], inc=1, device_id=y_dev, device_id_type=MESH)

    def again(i):
        rs = at(i * sub, sub)
        normal = (X[rs, :].astype(F32) - STAT[rs, 0:1]) * STAT[rs, 1:2]
        N[rs, :] = (normal * NV[0:1, :] + NV[1:2, :]).astype(BF16)

    tiles(rows_all // sub, again)
    TMP[...] = jnp.zeros_like(TMP)
    for i in range(cols):
        mine, span, low = key_range(i)
        query = QKV[mine, 0:HD]
        p = jnp.exp(block_scores(i) - STAT[mine, 2:3])
        d_p = dot(DAT[mine, :], QKV[span, 2 * HD :], NT)
        delta = jnp.sum(d_p * p, axis=1, keepdims=True)
        d_s = (p * (d_p - delta)).astype(BF16)
        p_low = p.astype(BF16)
        d_query = dot(d_s, QKV[span, HD : 2 * HD], NN) * scale
        QKV[mine, 0:HD] = rotate(d_query, mine, -1.0).astype(BF16)
        for j in range(low // blk, i + 1):
            js = slice(j * blk - low, (j + 1) * blk - low)
            ks, vs = slice(j * HD, (j + 1) * HD), slice((cols + j) * HD, (cols + j + 1) * HD)
            TMP[:, ks] += dot(d_s[:, js], query, TN)
            TMP[:, vs] += dot(p_low[:, js], DAT[mine, :], TN)
    for j in range(cols):
        mine = slice(j * blk, (j + 1) * blk)
        ks, vs = slice(j * HD, (j + 1) * HD), slice((cols + j) * HD, (cols + j + 1) * HD)
        QKV[mine, HD : 2 * HD] = rotate(TMP[:, ks] * scale, mine, -1.0).astype(BF16)
        QKV[mine, 2 * HD :] = TMP[:, vs].astype(BF16)

    in_give(
        "qk", QKV, give_h, hh, [SLOPE.at[:, pl.ds(0, hh)], SLOPE.at[:, pl.ds(hh, hh)]], S_qk
    )
    copies.came("dn1y")
    copies.start("dn1x", R_dn, X_dn.at[1], x_dev)
    in_keep("qk", 0, QKV, keep_h, S_qk)
    copies.start("qk0x", S_qk.at[0], X_qk[0], x_dev)
    in_keep("qk", 1, QKV, keep_h, S_qk)
    copies.start("qk1y", S_qk.at[1], R_qk, y_dev)

    def finish(name, total, came, result, here):
        copies.came(f"{name}x")
        n = total.shape[0]
        step = min(n, 128)

        def part(i):
            rs = at(i * step, step)
            came[rs, :] = (total[rs, :].astype(F32) + came[rs, :].astype(F32)).astype(BF16)

        tiles(n // step, part)
        fetch(came, result.at[here])
        copies.start(f"{name}t", came, result.at[here], core_dev)

    wide = slice(None)

    def down_at(side):
        return (at(side * units + k * uh, uh), wide)

    def dense_at(side):
        return (at(side * HD + k * dh, dh), wide)

    def up_at(side):
        return (wide, at(side * units + k * uh, uh))

    def qkv_at(side):
        return (wide, at(side * heads + k * hh, hh))

    finish("dn0", S_dn.at[0], X_dn.at[0], g_down, down_at(r))

    NSUM[...] = jnp.zeros_like(NSUM)
    pl.semaphore_wait(credit.at[2], 1)

    def norm_back(b):
        rb = rows(b)
        mean, inv = STAT[rb, 0:1], STAT[rb, 1:2]

        def first(j, carry):
            along, plain = carry
            cs = at(j * TILE, TILE)
            one = dot(QKV[rb, :], WQ[cs, :], NT)
            two = dot(DUP[rb, :], WU[cs, :], NT)
            normal = (X[rb, cs].astype(F32) - mean) * inv
            NSUM[0:1, cs] += jnp.sum(one * normal, axis=0, keepdims=True)
            NSUM[1:2, cs] += jnp.sum(one, axis=0, keepdims=True)
            NSUM[2:3, cs] += jnp.sum(two * normal, axis=0, keepdims=True)
            NSUM[3:4, cs] += jnp.sum(two, axis=0, keepdims=True)
            grad = one * NV[0:1, cs] + two * NV[2:3, cs]
            TMP[:, cs] = grad
            along = along + jnp.sum(grad * normal, axis=1, keepdims=True)
            plain = plain + jnp.sum(grad, axis=1, keepdims=True)
            return along, plain

        zero = jnp.zeros((blk, 1), F32)
        along, plain = lax.fori_loop(0, width // TILE, first, (zero, zero))
        along, plain = along * (1.0 / width), plain * (1.0 / width)

        def second(j):
            cs = at(j * TILE, TILE)
            normal = (X[rb, cs].astype(F32) - mean) * inv
            N[rb, cs] = (inv * (TMP[:, cs] - plain - normal * along)).astype(BF16)

        tiles(width // TILE, second)

    for s in (1, 2, 3, 0):
        norm_back(col_of[s])
        copies.start(
            f"ey{s}", N.at[rows(col_of[s]), other], HID.at[rows(col_of[s]), :], y_dev
        )
        if s == 1:
            copies.came("up1y")
            copies.start("up1x", R_up, X_up[1], x_dev)
        if s == 2:
            copies.came("de1y")
            copies.start("de1x", R_de, X_de.at[1], x_dev)

    SM[0:4, :] = NSUM[0:4, own]
    SM[4:5, :] = jnp.sum(DUP[...].astype(F32), axis=0, keepdims=True)
    SM[5:6, 0:heads] = jnp.sum(QKV[...].astype(F32), axis=0, keepdims=True)
    SM[5:6, heads:] = jnp.zeros((1, wid - heads), F32)
    SM[7:8, :] = jnp.zeros((1, wid), F32)
    SMO[0:4, :] = NSUM[0:4, other]
    SMO[4:8, :] = jnp.zeros((4, wid), F32)
    copies.start("s0", SMO, SMR.at[0], y_dev)

    def small_next(j, device, top):
        def action():
            copies.came(f"s{j - 1}")
            copies.sent(f"s{j - 1}")
            SM[0:top, :] = SM[0:top, :] + SMR[j - 1, 0:top, :]
            if device is not None:
                copies.start(f"s{j}", SM, SMR.at[j], device)

        return action

    mine = rows(c)
    for s in (1, 2, 3):
        copies.came(f"oz{s}")

    def branch_sum(part, columns):
        rs = at(part * sub, sub)
        total = OUTP[at(c * blk + part * sub, sub), columns].astype(F32)
        for s in (1, 2, 3):
            total = total + ORECV[s - 1, rs, columns].astype(F32)
        return total

    def out_other(i):
        OUTP[at(c * blk + i * sub, sub), other] = branch_sum(i, other).astype(BF16)

    tiles(blk // sub, out_other)
    copies.start("oy", OUTP.at[mine, other], OY, y_dev)

    def x_block(s):
        def action():
            b = col_of[s]
            copies.came(f"ey{s}")

            def part(i):
                rs = at(b * blk + i * sub, sub)
                N[rs, own] = (N[rs, own].astype(F32) + HID[rs, :].astype(F32)).astype(BF16)

            tiles(blk // sub, part)
            if s > 0:
                copies.start(f"ez{s}", N.at[rows(b), own], DZ.at[s - 1], {"col": b})

        return action

    def out_last():
        copies.came("oy")

        def part(i):
            rs = at(i * sub, sub)
            total = branch_sum(i, own) + OY[rs, :].astype(F32)
            total = total + X[at(c * blk + i * sub, sub), own].astype(F32)
            out[rs, :] = (total + (dense_b[...] + down_b[...])).astype(BF16)

        tiles(blk // sub, part)

    def x_last():
        for s in (1, 2, 3):
            copies.came(f"ez{s}")

        def part(i):
            rs = at(i * sub, sub)
            total = N[at(c * blk + i * sub, sub), own].astype(F32)
            for s in (1, 2, 3):
                total = total + DZ[s - 1, rs, :].astype(F32)
            in_grad[rs, :] = cot[rs, :].astype(F32) + total

        tiles(blk // sub, part)

    def send_qk():
        copies.came("qk1y")
        copies.start("qk1x", R_qk, X_qk[1], x_dev)

    finish("up0", S_up.at[0], X_up[0], g_up, up_at(r))
    small_next(1, {"col": col_of[1]}, 4)()
    finish("de0", S_de.at[0], X_de.at[0], g_dense, dense_at(r))
    send_qk()
    small_next(2, {"col": col_of[2]}, 4)()
    finish("dn1", R_dn, X_dn.at[1], g_down, down_at(1 - r))
    x_block(1)()
    small_next(3, core_dev, 4)()
    finish("qk0", S_qk.at[0], X_qk[0], g_qkv, qkv_at(r))
    x_block(2)()
    small_next(4, x_dev, 8)()
    x_block(3)()
    finish("up1", R_up, X_up[1], g_up, up_at(1 - r))
    small_next(5, None, 8)()
    copies.start("s5", SM, SMR.at[5], y_dev)
    x_block(0)()
    finish("de1", R_de, X_de.at[1], g_dense, dense_at(1 - r))
    out_last()
    copies.came("s5")
    small[0:8, :] = SM[...]
    small[8:16, :] = SMR[5]
    x_last()
    finish("qk1", R_qk, X_qk[1], g_qkv, qkv_at(1 - r))
    for name in ("dn0", "up0", "de0", "dn1", "qk0", "up1", "de1", "qk1"):
        copies.came(f"{name}t")
    for copy in local[6:]:
        copy.wait()
    copies.sent_all()


def scratch(blk, wid, cols, units, heads):
    tokens, width = blk * cols, 2 * wid
    low = [
        (tokens, width), (tokens, width), (width, heads), (width, units), (HD, width),
        (units, width), (tokens, width),
    ]
    V = pltpu.VMEM
    return (
        [V(shape, BF16) for shape in low]
        + [V((tokens, 128), F32)]
        + [
            V(shape, BF16)
            for shape in (
                (tokens, heads), (tokens, HD), (tokens, units), (tokens, units), (tokens, units),
                (tokens, HD), (tokens, width), (3, blk, width), (blk, wid), (3, blk, wid),
                (2, units // 2, wid), (2, HD // 2, wid), (2, wid, units // 2), (2, wid, heads // 2),
                (units // 2, wid), (HD // 2, wid), (2, units // 2, wid), (2, HD // 2, wid),
                (2, HD // 2, wid),
            )
        ]
        + [
            V((blk, width), F32),
            V((8, width), F32),
            V((tokens, 128), F32),
            V((tokens, 128), F32),
            V((8, width), F32),
            V((8, wid), F32),
            V((8, wid), F32),
            V((6, 8, wid), F32),
            pltpu.SemaphoreType.DMA((100,)),
            pltpu.SemaphoreType.DMA((100,)),
            pltpu.SemaphoreType.DMA((16,)),
            pltpu.SemaphoreType.REGULAR((3,)),
        ]
    )


def swap(value, axis, mask):
    size = lax.axis_size(axis)
    return lax.ppermute(value, axis, [(i, i ^ mask) for i in range(size)])


def shards(
    hidden_in,
    segment,
    norm1_gain,
    norm1_bias,
    norm2_gain,
    norm2_bias,
    qkv_weight,
    qkv_bias,
    dense_weight,
    dense_bias,
    up_weight,
    up_bias,
    down_weight,
    down_bias,
    cotangent,
):
    blk, wid = hidden_in.shape
    cols = lax.axis_size("col")
    heads, units = qkv_weight.shape[1] // 2, up_weight.shape[1] // 2
    vectors = [
        v.reshape(1, -1)
        for v in (
            norm1_gain, norm1_bias, norm2_gain, norm2_bias, qkv_bias, up_bias, dense_bias, down_bias,
        )
    ]
    vmem = pl.BlockSpec(memory_space=pltpu.VMEM)
    far = pl.BlockSpec(memory_space=pl.ANY)
    shape = jax.ShapeDtypeStruct
    out, in_grad, small, g_qkv, g_dense, g_up, g_down = pl.pallas_call(
        functools.partial(step_kernel, (blk, wid, cols)),
        out_shape=(
            shape((blk, wid), BF16),
            shape((blk, wid), F32),
            shape((16, wid), F32),
            shape(qkv_weight.shape, BF16),
            shape(dense_weight.shape, BF16),
            shape(up_weight.shape, BF16),
            shape(down_weight.shape, BF16),
        ),
        in_specs=[vmem, vmem] + [far] * 4 + [vmem] * 9,
        out_specs=(vmem,) * 3 + (far,) * 4,
        scratch_shapes=scratch(blk, wid, cols, units, heads),
        compiler_params=pltpu.CompilerParams(
            collective_id=0, has_side_effects=True, vmem_limit_bytes=67043328
        ),
        name="step",
    )(
        hidden_in, cotangent, qkv_weight, up_weight, dense_weight, down_weight, segment, *vectors
    )

    grads = [g.astype(F32) for g in (g_qkv, g_dense, g_up, g_down)]
    mask = 4
    while mask < lax.axis_size("dp"):
        grads = [g + swap(g.astype(BF16), "dp", mask).astype(F32) for g in grads]
        small = small + swap(small, "dp", mask)
        mask *= 2
    row = lax.axis_index("row")

    def both(index):
        first, second = small[index], small[8 + index]
        return jnp.where(row == 0, first, second), jnp.where(row == 0, second, first)

    qkv_bias_grad = jnp.concatenate([part[:heads] for part in both(5)])
    up_bias_grad = jnp.concatenate(both(4))
    return (
        out,
        in_grad,
        small[0],
        small[1],
        small[2],
        small[3],
        grads[0],
        qkv_bias_grad,
        grads[1],
        small[6],
        grads[2],
        up_bias_grad,
        grads[3],
        small[6],
    )


def solution(mesh):
    return jax.shard_map(
        shards,
        mesh=mesh,
        in_specs=(
            P(("dp", "col"), "row"),
            P("dp", None),
            P("row"),
            P("row"),
            P("row"),
            P("row"),
            P("row", "col"),
            P("col"),
            P("col", "row"),
            P("row"),
            P("row", "col"),
            P("col"),
            P("col", "row"),
            P("row"),
            P(("dp", "col"), "row"),
        ),
        out_specs=(
            P(("dp", "col"), "row"),
            P(("dp", "col"), "row"),
            P("row"),
            P("row"),
            P("row"),
            P("row"),
            P("row", "col"),
            P("col"),
            P("col", "row"),
            P("row"),
            P("row", "col"),
            P("col"),
            P("col", "row"),
            P("row"),
        ),
        check_vma=False,
    )
```

profile of v0, /device:TPU:9, one launch (start us, length us, event | category | flops | bytes accessed | tf_op | source)
XLA Modules:
  0.0 371.1 jit_solution(12243088233345788282)
XLA Ops:
  0.6 1.3 reshape.66.qkv_b
  1.9 347.5 %step.1 = (bf16[256,1024]{1,0:T(8,128)(2,1)}, f32[256,1024]{1,0:T(8,128)}, f32[16,1024]{1,0:T(8,128)}, bf16[1024,1536]{1,0:T(8,128)(2,1)}, bf16[512,1024]{1,0:T(...) custom-call(bf16[256,1024]{1,0:T(8,128)(2,1)} %hid.1, bf16[256,1024]{1,0:T(8,128)(2,1)} %cot.1, ...), custom_call_target="tpu_custom_call" | custom-call | tf_op jit(solution)/shard_map/step/pallas_call | solution.py:751
  349.4 1.7 broadcast_select_fusion
  351.1 0.0 copy-start.5
  351.1 0.6 pad_maximum_fusion
  351.7 0.6 pad_maximum_fusion.1
  352.3 0.0 copy-start
  352.3 6.8 %convert_element_type.14 = f32[1024,2048]{1,0:T(8,128)} convert(bf16[1024,2048]{1,0:T(8,128)(2,1)} %get-tuple-element.26) | non-fusion elementwise | flops 2097152 | bytes 12582912 | tf_op jit(solution)/shard_map/convert_element_type | solution.py:773
  359.1 0.0 copy-done
  359.1 0.0 copy-start.1
  359.1 4.4 %convert_element_type.15 = f32[2048,1024]{1,0:T(8,128)} convert(bf16[2048,1024]{1,0:T(8,128)(2,1)S(1)} %copy-done) | non-fusion elementwise | flops 2097152 | bytes 12582912 | tf_op jit(solution)/shard_map/convert_element_type | solution.py:773
  363.6 0.0 copy-done.1
  363.6 0.0 copy-start.2
  363.6 0.0 copy-start.4
  363.6 3.6 convert_element_type.12
  367.2 0.0 copy-start.3
  367.2 0.0 copy-done.2
  367.2 1.6 convert_element_type.13
  368.7 0.0 copy-done.5
  368.7 0.6 copy.32
  369.3 0.0 copy-done.4
  369.3 0.8 copy.33
  370.1 0.0 copy-done.3
  370.1 1.0 copy.34
  (1 shorter events, 0.0 us)
Async XLA Ops:
  351.1 17.6 %copy-start.5 = (f32[1,1024]{1,0:T(1,128)}, f32[1,1024]{1,0:T(1,128)S(1)}, u32[]{:S(2)}) copy-start(f32[1,1024]{1,0:T(1,128)S(1)} %get-tuple-element.31) | copy-start | bytes 12292
  352.3 6.8 %copy-start = (bf16[2048,1024]{1,0:T(8,128)(2,1)S(1)}, bf16[2048,1024]{1,0:T(8,128)(2,1)}, u32[]{:S(2)}) copy-start(bf16[2048,1024]{1,0:T(8,128)(2,1)} %get-tuple-element.27) | copy-start | bytes 12582916
  359.1 4.4 %copy-start.1 = (bf16[1024,1536]{1,0:T(8,128)(2,1)S(1)}, bf16[1024,1536]{1,0:T(8,128)(2,1)}, u32[]{:S(2)}) copy-start(bf16[1024,1536]{1,0:T(8,128)(2,1)} %get-tuple-element.24) | copy-start | bytes 9437188
  363.6 3.6 copy-start.2
  363.6 5.7 %copy-start.4 = (bf16[256,1024]{1,0:T(8,128)(2,1)S(1)}, bf16[256,1024]{1,0:T(8,128)(2,1)}, u32[]{:S(2)}) copy-start(bf16[256,1024]{1,0:T(8,128)(2,1)} %get-tuple-element.81) | copy-start | bytes 1572868
  367.2 3.0 copy-start.3
where the time goes:
time: 371 us
  Pallas kernels  347 us (94%)
  other arithmetic  19.3 us (5%)
    pallas_call x1, Pallas kernels, shards(): pl.pallas_call(functools.partial(step_kernel, (blk, wid, cols)), out_shap...  347 us
    convert_element_type x4, other arithmetic, shards(): grads = [g.astype(F32) for g in (g_qkv, g_dense, g_up, g_down)]  16.4 us

commit v1 on v0

--- a/solution.py
+++ b/solution.py
@@ -75,8 +75,8 @@
     sizes,
     hid, cot, wq, wu, wd, wn, seg, gain1, bias1, gain2, bias2, qkv_b, up_b, dense_b, down_b,
     out, in_grad, small, g_qkv, g_dense, g_up, g_down,
-    X, G, WQ, WU, WD, WN, N, STAT, QKV, ATT, HID, SLOPE, DUP, DAT, OUTP, ORECV, OY, DZ,
-    S_dn, S_de, S_up, S_qk, R_dn, R_de, X_dn, X_de, A_de, TMP, NV, COS, SIN, NSUM, SM, SMO, SMR,
+    X, G, WQ, WU, WD, WN, N, STAT, QKV, ATT, HID, SLOPE, DUP, DAT, OUTP, OZ1, OZ, OY, DZ1, DZ,
+    S_dn, S_de, S_up, S_qk, R_dn, R_de, V_dn, V_de, X_dn, X_de, A_de, TMP, NV, COS, SIN, NSUM, SM, SMO, SMR,
     send_sem, recv_sem, local_sem, credit,
 ):
     blk, wid, cols = sizes
@@ -142,16 +142,19 @@
 
     q2 = q + 2 - 4 * hi
 
-    def weight(name, source, full, row0, size, columns):
-        def place(quarter):
-            return full.at[at(row0 + quarter * size, size), columns]
-
-        copies.start(f"{name}y", source, place(q), y_dev)
+    def weight(name, source, full, row0, size, columns, spread):
+        share = q if spread else k
+
+        def place(index):
+            return full.at[at(row0 + index * size, size), columns]
+
+        copies.start(f"{name}y", source(at(share * size, size)), place(share), y_dev)
 
         def pass_on():
             copies.came(f"{name}y")
-            copies.start(f"{name}x", place(q), place(q), x_dev)
-            copies.start(f"{name}c", place(q), place(q), core_dev)
+            if spread:
+                copies.start(f"{name}x", place(q), place(q), x_dev)
+            copies.start(f"{name}c", place(share), place(share), core_dev)
 
         def pass_far():
             copies.came(f"{name}x")
@@ -159,7 +162,8 @@
 
         def done():
             copies.came(f"{name}c")
-            copies.came(f"{name}f")
+            if spread:
+                copies.came(f"{name}f")
 
         return pass_on, pass_far, done
 
@@ -168,9 +172,8 @@
     copies.start("xy0", hid, X.at[rows(c), other], y_dev)
     for j, vector in enumerate((gain1, bias1, gain2, bias2)):
         copies.start(f"nv{j}", vector, NV.at[pl.ds(j, 1), other], y_dev)
-    wq4, wn4, wd4 = wid // 4, units // 4, HD // 4
     wu_on, wu_far, wu_done = weight(
-        "wu", wu.at[at(q * wq4, wq4), at((1 - r) * units, units)], WU, wid, wq4, everything
+        "wu", lambda rs: wu.at[rs, at((1 - r) * units, units)], WU, wid, wid // 4, everything, True
     )
 
     seg_row = seg[...].astype(F32)
@@ -241,46 +244,50 @@
     chain_wait("x", 1)
     chain_send("x", 2, X, own)
     row_send("xy1", 1)
-    copies.start("gy", cot, G.at[rows(c), other], y_dev)
     wu_on()
     chain_wait("x", 2)
     chain_send("x", 3, X, own)
     row_send("xy2", 2)
     chain_send("g", 1, G, own, cot)
-    wu_far()
-    fetch_u.wait()
     for j in range(4):
         copies.came(f"nv{j}")
     copies.came("xy0")
     norm_block(col_of[0])
     chain_wait("x", 3)
     row_send("xy3", 3)
-    wq_on, wq_far, wq_done = weight(
-        "wq", wq.at[at(q * wq4, wq4), at((1 - r) * heads, heads)], WQ, wid, wq4, everything
+    copies.start("gy", cot, G.at[rows(c), other], y_dev)
+    wq_on, _, wq_done = weight(
+        "wq", lambda rs: wq.at[rs, at((1 - r) * heads, heads)], WQ, wid, wid // 2, everything, False
     )
-    wn_on, wn_far, wn_done = weight(
-        "wn", wn.at[at((1 - r) * units + q * wn4, wn4), :], WN, 0, wn4, other
+
+    def rows_of(ref, start, rs):
+        return ref.at[at(start + rs.start, rs.size), :]
+
+    wn_on, _, wn_done = weight(
+        "wn", lambda rs: rows_of(wn, (1 - r) * units, rs), WN, 0, units // 2, other, False
     )
-    wd_on, wd_far, wd_done = weight(
-        "wd", wd.at[at((1 - r) * HD + q * wd4, wd4), :], WD, 0, wd4, other
+    wd_on, _, wd_done = weight(
+        "wd", lambda rs: rows_of(wd, (1 - r) * HD, rs), WD, 0, HD // 2, other, False
     )
+    wu_far()
+    copies.came("xy1")
+    norm_block(col_of[1])
+    fetch_u.wait()
     wu_done()
     up_block(col_of[0])
-    copies.came("xy1")
-    norm_block(col_of[1])
     up_block(col_of[1])
     chain_wait("g", 1)
     chain_send("g", 2, G, own)
     copies.came("xy2")
     norm_block(col_of[2])
     up_block(col_of[2])
+    chain_wait("g", 2)
+    chain_send("g", 3, G, own)
     copies.came("xy3")
     norm_block(col_of[3])
-    chain_wait("g", 2)
-    chain_send("g", 3, G, own)
+    up_block(col_of[3])
     copies.came("gy")
     chain_send("h", 1, G, other)
-    up_block(col_of[3])
 
     def grad_send(name, staged, left, right, n_rows, n_cols, target):
         def part(i):
@@ -316,18 +323,81 @@
 
         tiles(wid // TILE, keep_part)
 
+    halves = {}
+
+    def cross(name, total, n_rows, landing):
+        half_rows = n_rows // 2
+        give, keep = at((1 - hi) * half_rows, half_rows), at(hi * half_rows, half_rows)
+        copies.start(f"{name}x", total.at[give, :], landing, x_dev)
+        halves[name] = (total.at[keep, :], landing)
+
+    def crossed(name, target):
+        mine, landing = halves[name]
+        copies.came(f"{name}x")
+        n = landing.shape[0]
+        step = min(n, 128)
+
+        def part(i):
+            rs = at(i * step, step)
+            landing[rs, :] = (mine[rs, :].astype(F32) + landing[rs, :].astype(F32)).astype(BF16)
+
+        tiles(n // step, part)
+        copies.start(f"{name}y", landing, target, y_dev)
+
+    def spread_out(name, came, result, here):
+        copies.came(f"{name}y")
+        copies.start(f"{name}g", came, result.at[here], x_dev)
+        copies.start(f"{name}t", came, result.at[here], core_dev)
+        fetch(came, result.at[here])
+
+    def pass_quarter(name, result, there):
+        copies.came(f"{name}g")
+        copies.start(f"{name}f", result.at[there], result.at[there], core_dev)
+
+    def finish(name, total, came, result, here):
+        copies.came(f"{name}x")
+        n = total.shape[0]
+        step = min(n, 128)
+
+        def part(i):
+            rs = at(i * step, step)
+            came[rs, :] = (total[rs, :].astype(F32) + came[rs, :].astype(F32)).astype(BF16)
+
+        tiles(n // step, part)
+        copies.start(f"{name}t", came, result.at[here], core_dev)
+        fetch(came, result.at[here])
+
+    wide = slice(None)
+
+    def down_at(side, part=None):
+        start, n = side * units + k * uh, uh
+        if part is not None:
+            start, n = start + part * (uh // 2), uh // 2
+        return (at(start, n), wide)
+
+    def dense_at(side, part=None):
+        start, n = side * HD + k * dh, dh
+        if part is not None:
+            start, n = start + part * (dh // 2), dh // 2
+        return (at(start, n), wide)
+
+    def up_at(side, part=None):
+        taken = wide if part is None else at(part * (wid // 2), wid // 2)
+        return (taken, at(side * units + k * uh, uh))
+
+    def qkv_at(side, part=None):
+        taken = wide if part is None else at(part * (wid // 2), wid // 2)
+        return (taken, at(side * heads + k * hh, hh))
+
     chain_wait("g", 3)
     out_grad("dn0", 0, HID, hid_keep, hid_send, DUP.at[pl.ds(0, uh), :], S_dn.at[0])
     out_keep("dn0", 0, HID, hid_keep, S_dn.at[0])
-    copies.start("dn0x", S_dn.at[0], X_dn.at[0], x_dev)
-
-    wq_on()
-    fetch_q.wait()
+    copies.start("dn0x", S_dn.at[0], X_dn, x_dev)
+
     chain_wait("h", 1)
     chain_send("h", 2, G, other)
-    wn_on()
-    wd_on()
-    wq_far()
+    fetch_q.wait()
+    wq_on()
     wq_done()
 
     def qkv_block(i):
@@ -340,8 +410,8 @@
             QKV[block, j * HD : (j + 1) * HD] = value.astype(BF16)
 
     tiles(cols, qkv_block)
-    wn_far()
-    wd_far()
+    chain_wait("h", 2)
+    chain_send("h", 3, G, other)
 
     def key_range(i):
         low = max(0, i - 2) * blk
@@ -365,12 +435,11 @@
         STAT[mine, 2:3] = largest + jnp.log(total)
         p_low = (p / total).astype(BF16)
         ATT[mine, :] = dot(p_low, QKV[span, 2 * HD :], NN).astype(BF16)
-    chain_wait("h", 2)
-    chain_send("h", 3, G, other)
+    out_grad("de0", 0, ATT, att_keep, att_send, A_de.at[0], S_de.at[0])
+    out_keep("de0", 0, ATT, att_keep, S_de.at[0])
+    copies.start("de0x", S_de.at[0], X_de, x_dev)
     fetch_n.wait()
     fetch_d.wait()
-    wn_done()
-    wd_done()
 
     def branch_block(b):
         def part(j):
@@ -381,17 +450,14 @@
         tiles(width // TILE, part)
 
     chain_wait("h", 3)
-    for s in (1, 2, 3):
-        branch_block(col_of[s])
-        copies.start(
-            f"oz{s}", OUTP.at[rows(col_of[s]), :], ORECV.at[s - 1], {"col": col_of[s]}
-        )
     out_grad("dn1", 1, HID, hid_keep, hid_send, DUP.at[pl.ds(uh, uh), :], S_dn.at[1])
-    out_grad("de0", 0, ATT, att_keep, att_send, A_de.at[0], S_de.at[0])
     out_grad("de1", 1, ATT, att_keep, att_send, A_de.at[1], S_de.at[1])
+    wn_on()
     out_keep("dn1", 1, HID, hid_keep, S_dn.at[1])
-    copies.start("dn1y", S_dn.at[1], R_dn, y_dev)
-    branch_block(col_of[0])
+    cross("dn1", S_dn.at[1], uh, V_dn)
+    out_keep("de1", 1, ATT, att_keep, S_de.at[1])
+    cross("de1", S_de.at[1], dh, V_de)
+    wn_done()
 
     copies.sent("dn0a", "dn1a")
 
@@ -428,32 +494,41 @@
         tiles(wid // TILE, part)
 
     in_give(
-        "up", DUP, give_u, uh, [HID.at[:, pl.ds(0, uh)], HID.at[:, pl.ds(uh, uh)]], S_up
+        "up", DUP, give_u, uh, [SLOPE.at[:, pl.ds(0, uh)], SLOPE.at[:, pl.ds(uh, uh)]], S_up
     )
+    wd_on()
+    wd_done()
     for i in range(cols):
         mine = slice(i * blk, (i + 1) * blk)
         DAT[mine, :] = dot(G[mine, :], WD[...], NT).astype(BF16)
     SM[6:7, :] = jnp.sum(G[:, own].astype(F32), axis=0, keepdims=True)
-    out_keep("de0", 0, ATT, att_keep, S_de.at[0])
-    out_keep("de1", 1, ATT, att_keep, S_de.at[1])
 
     copies.sent(*[f"{t}{w}{s}" for t in "gh" for w in "ud" for s in (1, 2, 3)])
-    copies.sent("wnx", "wnc", "wnf")
     pl.semaphore_signal(credit.at[0], inc=1, device_id=x_dev, device_id_type=MESH)
     pl.semaphore_signal(credit.at[1], inc=1, device_id=y_dev, device_id_type=MESH)
-    R_up, X_up = G.at[:, pl.ds(2 * uh, uh)], [G.at[:, pl.ds(j * uh, uh)] for j in (0, 1)]
-    R_qk, X_qk = WN.at[:, pl.ds(2 * hh, hh)], [WN.at[:, pl.ds(j * hh, hh)] for j in (0, 1)]
-
+    X_up, low, high = G.at[:, pl.ds(0, uh)], pl.ds(0, wid // 2), pl.ds(wid // 2, wid // 2)
+    V_up, R_up = G.at[low, pl.ds(uh, uh)], G.at[high, pl.ds(uh, uh)]
+    X_qk = WN.at[:, pl.ds(0, hh)]
+    V_qk, R_qk = WN.at[low, pl.ds(hh, hh)], WN.at[high, pl.ds(hh, hh)]
+
+    in_keep("up", 1, DUP, keep_u, S_up)
+    pl.semaphore_wait(credit.at[0], 1)
+    cross("up1", S_up.at[1], wid, V_up)
     in_keep("up", 0, DUP, keep_u, S_up)
-    pl.semaphore_wait(credit.at[0], 1)
-    copies.start("up0x", S_up.at[0], X_up[0], x_dev)
-    in_keep("up", 1, DUP, keep_u, S_up)
-    pl.semaphore_wait(credit.at[1], 1)
-    copies.start("up1y", S_up.at[1], R_up, y_dev)
-    copies.start("de0x", S_de.at[0], X_de.at[0], x_dev)
-    copies.start("de1y", S_de.at[1], R_de, y_dev)
-    copies.sent("up0a", "up1a")
-    pl.semaphore_signal(credit.at[2], inc=1, device_id=y_dev, device_id_type=MESH)
+    copies.start("up0x", S_up.at[0], X_up, x_dev)
+
+    crossed("dn1", R_dn)
+    for s in (2, 3):
+        branch_block(col_of[s])
+        copies.start(f"oy{s}", OUTP.at[rows(col_of[s]), other], OY.at[s - 1], y_dev)
+    crossed("de1", R_de)
+    branch_block(col_of[1])
+    copies.start("oz1", OUTP.at[rows(col_of[1]), :], OZ1, {"col": col_of[1]})
+    branch_block(col_of[0])
+    copies.sent("wnc")
+    pl.semaphore_signal(credit.at[2], inc=1, device_id=x_dev, device_id_type=MESH)
+    pl.semaphore_signal(credit.at[3], inc=1, device_id=y_dev, device_id_type=MESH)
+    pl.semaphore_signal(credit.at[4], inc=1, device_id=y_dev, device_id_type=MESH)
 
     def again(i):
         rs = at(i * sub, sub)
@@ -483,47 +558,37 @@
         QKV[mine, HD : 2 * HD] = rotate(TMP[:, ks] * scale, mine, -1.0).astype(BF16)
         QKV[mine, 2 * HD :] = TMP[:, vs].astype(BF16)
 
+    copies.sent("up0a", "up1a")
     in_give(
         "qk", QKV, give_h, hh, [SLOPE.at[:, pl.ds(0, hh)], SLOPE.at[:, pl.ds(hh, hh)]], S_qk
     )
-    copies.came("dn1y")
-    copies.start("dn1x", R_dn, X_dn.at[1], x_dev)
+    pl.semaphore_wait(credit.at[1], 1)
+    crossed("up1", R_up)
+    spread_out("dn1", R_dn, g_down, down_at(1 - r, hi))
+    in_keep("qk", 1, QKV, keep_h, S_qk)
+    pl.semaphore_wait(credit.at[2], 1)
+    cross("qk1", S_qk.at[1], wid, V_qk)
     in_keep("qk", 0, QKV, keep_h, S_qk)
-    copies.start("qk0x", S_qk.at[0], X_qk[0], x_dev)
-    in_keep("qk", 1, QKV, keep_h, S_qk)
-    copies.start("qk1y", S_qk.at[1], R_qk, y_dev)
-
-    def finish(name, total, came, result, here):
-        copies.came(f"{name}x")
-        n = total.shape[0]
-        step = min(n, 128)
+    copies.start("qk0x", S_qk.at[0], X_qk, x_dev)
+    finish("dn0", S_dn.at[0], X_dn, g_down, down_at(r))
+    finish("de0", S_de.at[0], X_de, g_dense, dense_at(r))
+
+    def out_block(s):
+        b = col_of[s]
+        copies.came(f"oy{s}")
 
         def part(i):
-            rs = at(i * step, step)
-            came[rs, :] = (total[rs, :].astype(F32) + came[rs, :].astype(F32)).astype(BF16)
-
-        tiles(n // step, part)
-        fetch(came, result.at[here])
-        copies.start(f"{name}t", came, result.at[here], core_dev)
-
-    wide = slice(None)
-
-    def down_at(side):
-        return (at(side * units + k * uh, uh), wide)
-
-    def dense_at(side):
-        return (at(side * HD + k * dh, dh), wide)
-
-    def up_at(side):
-        return (wide, at(side * units + k * uh, uh))
-
-    def qkv_at(side):
-        return (wide, at(side * heads + k * hh, hh))
-
-    finish("dn0", S_dn.at[0], X_dn.at[0], g_down, down_at(r))
+            rs = at(b * blk + i * sub, sub)
+            came = OY[s - 1, at(i * sub, sub), :]
+            OUTP[rs, own] = (OUTP[rs, own].astype(F32) + came.astype(F32)).astype(BF16)
+
+        tiles(blk // sub, part)
+        copies.start(f"oz{s}", OUTP.at[rows(b), own], OZ.at[s - 2], {"col": b})
+
+    out_block(2)
 
     NSUM[...] = jnp.zeros_like(NSUM)
-    pl.semaphore_wait(credit.at[2], 1)
+    pl.semaphore_wait(credit.at[4], 1)
 
     def norm_back(b):
         rb = rows(b)
@@ -556,17 +621,20 @@
 
         tiles(width // TILE, second)
 
-    for s in (1, 2, 3, 0):
+    EY = [HID.at[pl.ds(j * blk, blk), :] for j in range(3)]
+    pl.semaphore_wait(credit.at[3], 1)
+    for s in (2, 3):
         norm_back(col_of[s])
-        copies.start(
-            f"ey{s}", N.at[rows(col_of[s]), other], HID.at[rows(col_of[s]), :], y_dev
-        )
-        if s == 1:
-            copies.came("up1y")
-            copies.start("up1x", R_up, X_up[1], x_dev)
+        copies.start(f"ey{s}", N.at[rows(col_of[s]), other], EY[s - 1], y_dev)
         if s == 2:
-            copies.came("de1y")
-            copies.start("de1x", R_de, X_de.at[1], x_dev)
+            spread_out("de1", R_de, g_dense, dense_at(1 - r, hi))
+            out_block(3)
+        else:
+            crossed("qk1", R_qk)
+    norm_back(col_of[1])
+    copies.start("ez1", N.at[rows(col_of[1]), :], DZ1, {"col": col_of[1]})
+    spread_out("up1", R_up, g_up, up_at(1 - r, hi))
+    norm_back(col_of[0])
 
     SM[0:4, :] = NSUM[0:4, own]
     SM[4:5, :] = jnp.sum(DUP[...].astype(F32), axis=0, keepdims=True)
@@ -587,91 +655,81 @@
 
         return action
 
-    mine = rows(c)
-    for s in (1, 2, 3):
-        copies.came(f"oz{s}")
-
-    def branch_sum(part, columns):
-        rs = at(part * sub, sub)
-        total = OUTP[at(c * blk + part * sub, sub), columns].astype(F32)
-        for s in (1, 2, 3):
-            total = total + ORECV[s - 1, rs, columns].astype(F32)
-        return total
-
-    def out_other(i):
-        OUTP[at(c * blk + i * sub, sub), other] = branch_sum(i, other).astype(BF16)
-
-    tiles(blk // sub, out_other)
-    copies.start("oy", OUTP.at[mine, other], OY, y_dev)
-
-    def x_block(s):
-        def action():
-            b = col_of[s]
-            copies.came(f"ey{s}")
-
-            def part(i):
-                rs = at(b * blk + i * sub, sub)
-                N[rs, own] = (N[rs, own].astype(F32) + HID[rs, :].astype(F32)).astype(BF16)
-
-            tiles(blk // sub, part)
-            if s > 0:
-                copies.start(f"ez{s}", N.at[rows(b), own], DZ.at[s - 1], {"col": b})
-
-        return action
-
-    def out_last():
-        copies.came("oy")
+    def mine_at(i):
+        return at(c * blk + i * sub, sub)
+
+    def row_rest(buf, came, landing, name):
+        copies.came(f"{name}z1")
 
         def part(i):
             rs = at(i * sub, sub)
-            total = branch_sum(i, own) + OY[rs, :].astype(F32)
-            total = total + X[at(c * blk + i * sub, sub), own].astype(F32)
-            out[rs, :] = (total + (dense_b[...] + down_b[...])).astype(BF16)
+            total = buf[mine_at(i), other].astype(F32) + came[rs, other].astype(F32)
+            buf[mine_at(i), other] = total.astype(BF16)
 
         tiles(blk // sub, part)
-
-    def x_last():
-        for s in (1, 2, 3):
-            copies.came(f"ez{s}")
+        copies.start(f"{name}y0", buf.at[rows(c), other], landing, y_dev)
+
+    def total_of(i, buf, near, far_ones, from_row):
+        rs = at(i * sub, sub)
+        total = buf[mine_at(i), own].astype(F32) + near[rs, own].astype(F32)
+        for ref in far_ones:
+            total = total + ref[rs, :].astype(F32)
+        return total + from_row[rs, :].astype(F32)
+
+    def x_block(s):
+        b = col_of[s]
+        copies.came(f"ey{s}")
 
         def part(i):
-            rs = at(i * sub, sub)
-            total = N[at(c * blk + i * sub, sub), own].astype(F32)
-            for s in (1, 2, 3):
-                total = total + DZ[s - 1, rs, :].astype(F32)
-            in_grad[rs, :] = cot[rs, :].astype(F32) + total
+            rs = at(b * blk + i * sub, sub)
+            came = EY[s - 1][at(i * sub, sub), :]
+            N[rs, own] = (N[rs, own].astype(F32) + came.astype(F32)).astype(BF16)
 
         tiles(blk // sub, part)
-
-    def send_qk():
-        copies.came("qk1y")
-        copies.start("qk1x", R_qk, X_qk[1], x_dev)
-
-    finish("up0", S_up.at[0], X_up[0], g_up, up_at(r))
+        copies.start(f"ez{s}", N.at[rows(b), own], DZ.at[s - 2], {"col": b})
+
+    row_rest(OUTP, OZ1, OY.at[0], "o")
     small_next(1, {"col": col_of[1]}, 4)()
-    finish("de0", S_de.at[0], X_de.at[0], g_dense, dense_at(r))
-    send_qk()
+    finish("up0", S_up.at[0], X_up, g_up, up_at(r))
+    pass_quarter("dn1", g_down, down_at(1 - r, 1 - hi))
+    pass_quarter("de1", g_dense, dense_at(1 - r, 1 - hi))
     small_next(2, {"col": col_of[2]}, 4)()
-    finish("dn1", R_dn, X_dn.at[1], g_down, down_at(1 - r))
-    x_block(1)()
+    x_block(2)
+    row_rest(N, DZ1, EY[0], "e")
+    x_block(3)
     small_next(3, core_dev, 4)()
-    finish("qk0", S_qk.at[0], X_qk[0], g_qkv, qkv_at(r))
-    x_block(2)()
+    spread_out("qk1", R_qk, g_qkv, qkv_at(1 - r, hi))
     small_next(4, x_dev, 8)()
-    x_block(3)()
-    finish("up1", R_up, X_up[1], g_up, up_at(1 - r))
+    finish("qk0", S_qk.at[0], X_qk, g_qkv, qkv_at(r))
     small_next(5, None, 8)()
     copies.start("s5", SM, SMR.at[5], y_dev)
-    x_block(0)()
-    finish("de1", R_de, X_de.at[1], g_dense, dense_at(1 - r))
-    out_last()
+    pass_quarter("up1", g_up, up_at(1 - r, 1 - hi))
+    for name in ("oz2", "oz3", "oy0"):
+        copies.came(name)
+
+    def out_last(i):
+        total = total_of(i, OUTP, OZ1, [OZ.at[0], OZ.at[1]], OY.at[0])
+        total = total + X[mine_at(i), own].astype(F32)
+        out[at(i * sub, sub), :] = (total + (dense_b[...] + down_b[...])).astype(BF16)
+
+    tiles(blk // sub, out_last)
     copies.came("s5")
     small[0:8, :] = SM[...]
     small[8:16, :] = SMR[5]
-    x_last()
-    finish("qk1", R_qk, X_qk[1], g_qkv, qkv_at(1 - r))
-    for name in ("dn0", "up0", "de0", "dn1", "qk0", "up1", "de1", "qk1"):
+    for name in ("ez2", "ez3", "ey0"):
+        copies.came(name)
+
+    def x_last(i):
+        total = total_of(i, N, DZ1, [DZ.at[0], DZ.at[1]], EY[0])
+        in_grad[at(i * sub, sub), :] = cot[at(i * sub, sub), :].astype(F32) + total
+
+    tiles(blk // sub, x_last)
+    pass_quarter("qk1", g_qkv, qkv_at(1 - r, 1 - hi))
+    for name in ("dn0", "de0", "up0", "qk0"):
         copies.came(f"{name}t")
+    for name in ("dn1", "de1", "up1", "qk1"):
+        copies.came(f"{name}t")
+        copies.came(f"{name}f")
     for copy in local[6:]:
         copy.wait()
     copies.sent_all()
@@ -691,10 +749,11 @@
             V(shape, BF16)
             for shape in (
                 (tokens, heads), (tokens, HD), (tokens, units), (tokens, units), (tokens, units),
-                (tokens, HD), (tokens, width), (3, blk, width), (blk, wid), (3, blk, wid),
+                (tokens, HD), (tokens, width), (blk, width), (2, blk, wid), (3, blk, wid),
+                (blk, width), (2, blk, wid),
                 (2, units // 2, wid), (2, HD // 2, wid), (2, wid, units // 2), (2, wid, heads // 2),
-                (units // 2, wid), (HD // 2, wid), (2, units // 2, wid), (2, HD // 2, wid),
-                (2, HD // 2, wid),
+                (units // 4, wid), (HD // 4, wid), (units // 4, wid), (HD // 4, wid),
+                (units // 2, wid), (HD // 2, wid), (2, HD // 2, wid),
             )
         ]
         + [
@@ -706,10 +765,10 @@
             V((8, wid), F32),
             V((8, wid), F32),
             V((6, 8, wid), F32),
-            pltpu.SemaphoreType.DMA((100,)),
-            pltpu.SemaphoreType.DMA((100,)),
-            pltpu.SemaphoreType.DMA((16,)),
-            pltpu.SemaphoreType.REGULAR((3,)),
+            pltpu.SemaphoreType.DMA((120,)),
+            pltpu.SemaphoreType.DMA((120,)),
+            pltpu.SemaphoreType.DMA((20,)),
+            pltpu.SemaphoreType.REGULAR((5,)),
         ]
     )
 

time: 371 us -> 294 us (0.79)
  Pallas kernels: 347 us -> 270 us
    pallas_call x1, Pallas kernels: 347 us -> 270 us  [shards(): pl.pallas_call(functools.partial(step_kernel, (blk, wid, cols)), out_shap...]
where the time goes in v1:
time: 294 us
  Pallas kernels  270 us (92%)
  other arithmetic  19.3 us (7%)
  local copies, waits for them, and re-layouts  3.67 us (1%)
    pallas_call x1, Pallas kernels, shards(): pl.pallas_call(functools.partial(step_kernel, (blk, wid, cols)), out_shap...  270 us
    convert_element_type x4, other arithmetic, shards(): grads = [g.astype(F32) for g in (g_qkv, g_dense, g_up, g_down)]  16.4 us

profile of v1, /device:TPU:9, one launch (start us, length us, event | category | flops | bytes accessed | tf_op | source)
XLA Modules:
  0.0 293.5 jit_solution(15809297017110734235)
XLA Ops:
  0.6 1.3 reshape.66.qkv_b
  1.9 269.9 %step.1 = (bf16[256,1024]{1,0:T(8,128)(2,1)}, f32[256,1024]{1,0:T(8,128)}, f32[16,1024]{1,0:T(8,128)}, bf16[1024,1536]{1,0:T(8,128)(2,1)}, bf16[512,1024]{1,0:T(...) custom-call(bf16[256,1024]{1,0:T(8,128)(2,1)} %hid.1, bf16[256,1024]{1,0:T(8,128)(2,1)} %cot.1, ...), custom_call_target="tpu_custom_call" | custom-call | tf_op jit(solution)/shard_map/step/pallas_call | solution.py:810
  271.8 1.7 broadcast_select_fusion
  273.5 0.0 copy-start.5
  273.5 0.6 pad_maximum_fusion
  274.1 0.6 pad_maximum_fusion.1
  274.7 0.0 copy-start
  274.7 6.8 %convert_element_type.14 = f32[1024,2048]{1,0:T(8,128)} convert(bf16[1024,2048]{1,0:T(8,128)(2,1)} %get-tuple-element.26) | non-fusion elementwise | flops 2097152 | bytes 12582912 | tf_op jit(solution)/shard_map/convert_element_type | solution.py:832
  281.5 0.0 copy-done
  281.5 0.0 copy-start.1
  281.5 4.4 %convert_element_type.15 = f32[2048,1024]{1,0:T(8,128)} convert(bf16[2048,1024]{1,0:T(8,128)(2,1)S(1)} %copy-done) | non-fusion elementwise | flops 2097152 | bytes 12582912 | tf_op jit(solution)/shard_map/convert_element_type | solution.py:832
  286.0 0.0 copy-done.1
  286.0 0.0 copy-start.2
  286.0 0.0 copy-start.4
  286.0 3.6 %convert_element_type.12 = f32[1024,1536]{1,0:T(8,128)} convert(bf16[1024,1536]{1,0:T(8,128)(2,1)S(1)} %copy-done.1) | non-fusion elementwise | flops 1572864 | bytes 9437184 | tf_op jit(solution)/shard_map/convert_element_type | solution.py:832
  289.6 0.0 copy-start.3
  289.6 0.0 copy-done.2
  289.6 1.6 convert_element_type.13
  291.1 0.0 copy-done.5
  291.1 0.6 copy.32
  291.7 0.0 copy-done.4
  291.7 0.8 copy.33
  292.5 0.0 copy-done.3
  292.5 1.0 copy.34
  (1 shorter events, 0.0 us)
Async XLA Ops:
  273.5 17.6 %copy-start.5 = (f32[1,1024]{1,0:T(1,128)}, f32[1,1024]{1,0:T(1,128)S(1)}, u32[]{:S(2)}) copy-start(f32[1,1024]{1,0:T(1,128)S(1)} %get-tuple-element.31) | copy-start | bytes 12292
  274.7 6.8 %copy-start = (bf16[2048,1024]{1,0:T(8,128)(2,1)S(1)}, bf16[2048,1024]{1,0:T(8,128)(2,1)}, u32[]{:S(2)}) copy-start(bf16[2048,1024]{1,0:T(8,128)(2,1)} %get-tuple-element.27) | copy-start | bytes 12582916
  281.5 4.4 %copy-start.1 = (bf16[1024,1536]{1,0:T(8,128)(2,1)S(1)}, bf16[1024,1536]{1,0:T(8,128)(2,1)}, u32[]{:S(2)}) copy-start(bf16[1024,1536]{1,0:T(8,128)(2,1)} %get-tuple-element.24) | copy-start | bytes 9437188
  286.0 3.6 %copy-start.2 = (bf16[512,1024]{1,0:T(8,128)(2,1)S(1)}, bf16[512,1024]{1,0:T(8,128)(2,1)}, u32[]{:S(2)}) copy-start(bf16[512,1024]{1,0:T(8,128)(2,1)} %get-tuple-element.25) | copy-start | bytes 3145732
  286.0 5.7 %copy-start.4 = (bf16[256,1024]{1,0:T(8,128)(2,1)S(1)}, bf16[256,1024]{1,0:T(8,128)(2,1)}, u32[]{:S(2)}) copy-start(bf16[256,1024]{1,0:T(8,128)(2,1)} %get-tuple-element.81) | copy-start | bytes 1572868
  289.6 3.0 %copy-start.3 = (f32[256,1024]{1,0:T(8,128)S(1)}, f32[256,1024]{1,0:T(8,128)}, u32[]{:S(2)}) copy-start(f32[256,1024]{1,0:T(8,128)} %get-tuple-element.82) | copy-start | bytes 3145732

commit v2 on v1

--- a/solution.py
+++ b/solution.py
@@ -76,7 +76,7 @@
     hid, cot, wq, wu, wd, wn, seg, gain1, bias1, gain2, bias2, qkv_b, up_b, dense_b, down_b,
     out, in_grad, small, g_qkv, g_dense, g_up, g_down,
     X, G, WQ, WU, WD, WN, N, STAT, QKV, ATT, HID, SLOPE, DUP, DAT, OUTP, OZ1, OZ, OY, DZ1, DZ,
-    S_dn, S_de, S_up, S_qk, R_dn, R_de, V_dn, V_de, X_dn, X_de, A_de, TMP, NV, COS, SIN, NSUM, SM, SMO, SMR,
+    S_dn, S_de, S_up, S_qk, R_dn, R_de, V_dn, V_de, X_dn, X_de, A_de, TMP, NV, COS, SIN, NSUM, SMO, SMR, NZ, NQ, BQ, BS, BR,
     send_sem, recv_sem, local_sem, credit,
 ):
     blk, wid, cols = sizes
@@ -92,6 +92,7 @@
     q = k + 2 * hi
     core_dev = {"dp": dp + 1 - 2 * k}
     x_dev = {"dp": dp + 2 - 4 * hi}
+    far_dev = {"dp": dp + 3 - 2 * k - 4 * hi}
     y_dev = {"row": 1 - r}
     c_low, c_high = lax.rem(c, 2), lax.div(c, 2)
     col_of = [c, c + 1 - 2 * c_low, c + 2 - 4 * c_high, 3 - c]
@@ -100,7 +101,7 @@
     copies = Copies(send_sem, recv_sem)
 
     barrier = pltpu.get_barrier_semaphore()
-    friends = [core_dev, x_dev, y_dev] + [{"col": col_of[s]} for s in (1, 2, 3)]
+    friends = [core_dev, x_dev, far_dev, y_dev] + [{"col": col_of[s]} for s in (1, 2, 3)]
     for device in friends:
         pl.semaphore_signal(barrier, inc=1, device_id=device, device_id_type=MESH)
 
@@ -263,8 +264,8 @@
     def rows_of(ref, start, rs):
         return ref.at[at(start + rs.start, rs.size), :]
 
-    wn_on, _, wn_done = weight(
-        "wn", lambda rs: rows_of(wn, (1 - r) * units, rs), WN, 0, units // 2, other, False
+    wn_on, wn_far, wn_done = weight(
+        "wn", lambda rs: rows_of(wn, (1 - r) * units, rs), WN, 0, units // 4, other, True
     )
     wd_on, _, wd_done = weight(
         "wd", lambda rs: rows_of(wd, (1 - r) * HD, rs), WD, 0, HD // 2, other, False
@@ -436,28 +437,39 @@
         p_low = (p / total).astype(BF16)
         ATT[mine, :] = dot(p_low, QKV[span, 2 * HD :], NN).astype(BF16)
     out_grad("de0", 0, ATT, att_keep, att_send, A_de.at[0], S_de.at[0])
-    out_keep("de0", 0, ATT, att_keep, S_de.at[0])
-    copies.start("de0x", S_de.at[0], X_de, x_dev)
     fetch_n.wait()
     fetch_d.wait()
 
-    def branch_block(b):
+    def branch_block(b, side):
         def part(j):
-            cs = at(j * TILE, TILE)
+            cs = at(side * wid + j * TILE, TILE)
             both = dot(ATT[rows(b), :], WD[:, cs], NN) + dot(HID[rows(b), :], WN[:, cs], NN)
             OUTP[rows(b), cs] = both.astype(BF16)
 
-        tiles(width // TILE, part)
+        tiles(wid // TILE, part)
+
+    tiles(cols, lambda b: branch_block(b, 0))
+    wn_on()
+    out_keep("de0", 0, ATT, att_keep, S_de.at[0])
 
     chain_wait("h", 3)
     out_grad("dn1", 1, HID, hid_keep, hid_send, DUP.at[pl.ds(uh, uh), :], S_dn.at[1])
     out_grad("de1", 1, ATT, att_keep, att_send, A_de.at[1], S_de.at[1])
-    wn_on()
+    wd_on()
     out_keep("dn1", 1, HID, hid_keep, S_dn.at[1])
     cross("dn1", S_dn.at[1], uh, V_dn)
     out_keep("de1", 1, ATT, att_keep, S_de.at[1])
     cross("de1", S_de.at[1], dh, V_de)
+    copies.start("de0x", S_de.at[0], X_de, x_dev)
+    wd_done()
+    wn_far()
     wn_done()
+    for s in (2, 3):
+        branch_block(col_of[s], 1)
+        copies.start(f"oy{s}", OUTP.at[rows(col_of[s]), other], OY.at[s - 1], y_dev)
+    branch_block(col_of[1], 1)
+    copies.start("oz1", OUTP.at[rows(col_of[1]), :], OZ1, {"col": col_of[1]})
+    branch_block(col_of[0], 1)
 
     copies.sent("dn0a", "dn1a")
 
@@ -496,12 +508,10 @@
     in_give(
         "up", DUP, give_u, uh, [SLOPE.at[:, pl.ds(0, uh)], SLOPE.at[:, pl.ds(uh, uh)]], S_up
     )
-    wd_on()
-    wd_done()
     for i in range(cols):
         mine = slice(i * blk, (i + 1) * blk)
         DAT[mine, :] = dot(G[mine, :], WD[...], NT).astype(BF16)
-    SM[6:7, :] = jnp.sum(G[:, own].astype(F32), axis=0, keepdims=True)
+    BQ[q, 2:3, :] = jnp.sum(G[:, own].astype(F32), axis=0, keepdims=True)
 
     copies.sent(*[f"{t}{w}{s}" for t in "gh" for w in "ud" for s in (1, 2, 3)])
     pl.semaphore_signal(credit.at[0], inc=1, device_id=x_dev, device_id_type=MESH)
@@ -518,17 +528,25 @@
     copies.start("up0x", S_up.at[0], X_up, x_dev)
 
     crossed("dn1", R_dn)
-    for s in (2, 3):
-        branch_block(col_of[s])
-        copies.start(f"oy{s}", OUTP.at[rows(col_of[s]), other], OY.at[s - 1], y_dev)
     crossed("de1", R_de)
-    branch_block(col_of[1])
-    copies.start("oz1", OUTP.at[rows(col_of[1]), :], OZ1, {"col": col_of[1]})
-    branch_block(col_of[0])
-    copies.sent("wnc")
+    copies.sent("wnx", "wnc", "wnf")
     pl.semaphore_signal(credit.at[2], inc=1, device_id=x_dev, device_id_type=MESH)
     pl.semaphore_signal(credit.at[3], inc=1, device_id=y_dev, device_id_type=MESH)
     pl.semaphore_signal(credit.at[4], inc=1, device_id=y_dev, device_id_type=MESH)
+
+    def out_block(s):
+        b = col_of[s]
+        copies.came(f"oy{s}")
+
+        def part(i):
+            rs = at(b * blk + i * sub, sub)
+            came = OY[s - 1, at(i * sub, sub), :]
+            OUTP[rs, own] = (OUTP[rs, own].astype(F32) + came.astype(F32)).astype(BF16)
+
+        tiles(blk // sub, part)
+        copies.start(f"oz{s}", OUTP.at[rows(b), own], OZ.at[s - 2], {"col": b})
+
+    out_block(2)
 
     def again(i):
         rs = at(i * sub, sub)
@@ -536,6 +554,7 @@
         N[rs, :] = (normal * NV[0:1, :] + NV[1:2, :]).astype(BF16)
 
     tiles(rows_all // sub, again)
+    out_block(3)
     TMP[...] = jnp.zeros_like(TMP)
     for i in range(cols):
         mine, span, low = key_range(i)
@@ -564,28 +583,26 @@
     )
     pl.semaphore_wait(credit.at[1], 1)
     crossed("up1", R_up)
-    spread_out("dn1", R_dn, g_down, down_at(1 - r, hi))
     in_keep("qk", 1, QKV, keep_h, S_qk)
     pl.semaphore_wait(credit.at[2], 1)
     cross("qk1", S_qk.at[1], wid, V_qk)
     in_keep("qk", 0, QKV, keep_h, S_qk)
     copies.start("qk0x", S_qk.at[0], X_qk, x_dev)
-    finish("dn0", S_dn.at[0], X_dn, g_down, down_at(r))
-    finish("de0", S_de.at[0], X_de, g_dense, dense_at(r))
-
-    def out_block(s):
-        b = col_of[s]
-        copies.came(f"oy{s}")
-
-        def part(i):
-            rs = at(b * blk + i * sub, sub)
-            came = OY[s - 1, at(i * sub, sub), :]
-            OUTP[rs, own] = (OUTP[rs, own].astype(F32) + came.astype(F32)).astype(BF16)
-
-        tiles(blk // sub, part)
-        copies.start(f"oz{s}", OUTP.at[rows(b), own], OZ.at[s - 2], {"col": b})
-
-    out_block(2)
+
+    def gather_dp(name, slots):
+        for word, device in (("c", core_dev), ("x", x_dev), ("d", far_dev)):
+            copies.start(f"{name}{word}", slots.at[q], slots.at[q], device)
+
+    def gathered_dp(name, slots):
+        for word in "cxd":
+            copies.came(f"{name}{word}")
+        return slots[0] + slots[1] + slots[2] + slots[3]
+
+    BQ[q, 0:1, :] = jnp.sum(DUP[...].astype(F32), axis=0, keepdims=True)
+    BQ[q, 1:2, 0:heads] = jnp.sum(QKV[...].astype(F32), axis=0, keepdims=True)
+    BQ[q, 1:2, heads:] = jnp.zeros((1, wid - heads), F32)
+    BQ[q, 3:8, :] = jnp.zeros((5, wid), F32)
+    gather_dp("b", BQ)
 
     NSUM[...] = jnp.zeros_like(NSUM)
     pl.semaphore_wait(credit.at[4], 1)
@@ -627,33 +644,14 @@
         norm_back(col_of[s])
         copies.start(f"ey{s}", N.at[rows(col_of[s]), other], EY[s - 1], y_dev)
         if s == 2:
+            spread_out("dn1", R_dn, g_down, down_at(1 - r, hi))
+        else:
             spread_out("de1", R_de, g_dense, dense_at(1 - r, hi))
-            out_block(3)
-        else:
-            crossed("qk1", R_qk)
     norm_back(col_of[1])
     copies.start("ez1", N.at[rows(col_of[1]), :], DZ1, {"col": col_of[1]})
-    spread_out("up1", R_up, g_up, up_at(1 - r, hi))
     norm_back(col_of[0])
-
-    SM[0:4, :] = NSUM[0:4, own]
-    SM[4:5, :] = jnp.sum(DUP[...].astype(F32), axis=0, keepdims=True)
-    SM[5:6, 0:heads] = jnp.sum(QKV[...].astype(F32), axis=0, keepdims=True)
-    SM[5:6, heads:] = jnp.zeros((1, wid - heads), F32)
-    SM[7:8, :] = jnp.zeros((1, wid), F32)
     SMO[0:4, :] = NSUM[0:4, other]
-    SMO[4:8, :] = jnp.zeros((4, wid), F32)
-    copies.start("s0", SMO, SMR.at[0], y_dev)
-
-    def small_next(j, device, top):
-        def action():
-            copies.came(f"s{j - 1}")
-            copies.sent(f"s{j - 1}")
-            SM[0:top, :] = SM[0:top, :] + SMR[j - 1, 0:top, :]
-            if device is not None:
-                copies.start(f"s{j}", SM, SMR.at[j], device)
-
-        return action
+    copies.start("sy", SMO, SMR, y_dev)
 
     def mine_at(i):
         return at(c * blk + i * sub, sub)
@@ -689,21 +687,28 @@
         copies.start(f"ez{s}", N.at[rows(b), own], DZ.at[s - 2], {"col": b})
 
     row_rest(OUTP, OZ1, OY.at[0], "o")
-    small_next(1, {"col": col_of[1]}, 4)()
+    spread_out("up1", R_up, g_up, up_at(1 - r, hi))
+    finish("dn0", S_dn.at[0], X_dn, g_down, down_at(r))
+    finish("de0", S_de.at[0], X_de, g_dense, dense_at(r))
     finish("up0", S_up.at[0], X_up, g_up, up_at(r))
+    crossed("qk1", R_qk)
+    x_block(2)
+    copies.came("sy")
+    NZ[c, 0:4, :] = NSUM[0:4, own] + SMR[0:4, :]
+    for s in (1, 2, 3):
+        copies.start(f"sz{s}", NZ.at[c], NZ.at[c], {"col": col_of[s]})
+    x_block(3)
+    row_rest(N, DZ1, EY[0], "e")
+    BS[...] = gathered_dp("b", BQ)
+    copies.start("by", BS, BR, y_dev)
+    finish("qk0", S_qk.at[0], X_qk, g_qkv, qkv_at(r))
+    for s in (1, 2, 3):
+        copies.came(f"sz{s}")
+    NQ[q] = NZ[0] + NZ[1] + NZ[2] + NZ[3]
+    gather_dp("n", NQ)
     pass_quarter("dn1", g_down, down_at(1 - r, 1 - hi))
     pass_quarter("de1", g_dense, dense_at(1 - r, 1 - hi))
-    small_next(2, {"col": col_of[2]}, 4)()
-    x_block(2)
-    row_rest(N, DZ1, EY[0], "e")
-    x_block(3)
-    small_next(3, core_dev, 4)()
     spread_out("qk1", R_qk, g_qkv, qkv_at(1 - r, hi))
-    small_next(4, x_dev, 8)()
-    finish("qk0", S_qk.at[0], X_qk, g_qkv, qkv_at(r))
-    small_next(5, None, 8)()
-    copies.start("s5", SM, SMR.at[5], y_dev)
-    pass_quarter("up1", g_up, up_at(1 - r, 1 - hi))
     for name in ("oz2", "oz3", "oy0"):
         copies.came(name)
 
@@ -713,9 +718,11 @@
         out[at(i * sub, sub), :] = (total + (dense_b[...] + down_b[...])).astype(BF16)
 
     tiles(blk // sub, out_last)
-    copies.came("s5")
-    small[0:8, :] = SM[...]
-    small[8:16, :] = SMR[5]
+    pass_quarter("up1", g_up, up_at(1 - r, 1 - hi))
+    copies.came("by")
+    small[0:8, :] = BS[...]
+    small[8:16, :] = BR[...]
+    small[4:8, :] = gathered_dp("n", NQ)[0:4]
     for name in ("ez2", "ez3", "ey0"):
         copies.came(name)
 
@@ -764,7 +771,11 @@
             V((8, width), F32),
             V((8, wid), F32),
             V((8, wid), F32),
-            V((6, 8, wid), F32),
+            V((cols, 8, wid), F32),
+            V((4, 8, wid), F32),
+            V((4, 8, wid), F32),
+            V((8, wid), F32),
+            V((8, wid), F32),
             pltpu.SemaphoreType.DMA((120,)),
             pltpu.SemaphoreType.DMA((120,)),
             pltpu.SemaphoreType.DMA((20,)),
@@ -841,23 +852,23 @@
         first, second = small[index], small[8 + index]
         return jnp.where(row == 0, first, second), jnp.where(row == 0, second, first)
 
-    qkv_bias_grad = jnp.concatenate([part[:heads] for part in both(5)])
-    up_bias_grad = jnp.concatenate(both(4))
+    qkv_bias_grad = jnp.concatenate([part[:heads] for part in both(1)])
+    up_bias_grad = jnp.concatenate(both(0))
     return (
         out,
         in_grad,
-        small[0],
-        small[1],
-        small[2],
-        small[3],
+        small[4],
+        small[5],
+        small[6],
+        small[7],
         grads[0],
         qkv_bias_grad,
         grads[1],
-        small[6],
+        small[2],
         grads[2],
         up_bias_grad,
         grads[3],
-        small[6],
+        small[2],
     )
 
 

time: 294 us -> 265 us (0.901)
  Pallas kernels: 270 us -> 240 us
    pallas_call x1, Pallas kernels: 270 us -> 240 us  [shards(): pl.pallas_call(functools.partial(step_kernel, (blk, wid, cols)), out_shap...]
where the time goes in v2:
time: 265 us; the launch traced here: 263 us
  Pallas kernels  240 us (91%)
  other arithmetic  19.3 us (7%)
  local copies, waits for them, and re-layouts  3.67 us (1%)
    pallas_call x1, Pallas kernels, shards(): pl.pallas_call(functools.partial(step_kernel, (blk, wid, cols)), out_shap...  240 us
    convert_element_type x4, other arithmetic, shards(): grads = [g.astype(F32) for g in (g_qkv, g_dense, g_up, g_down)]  16.4 us

profile of v2, /device:TPU:9, one launch (start us, length us, event | category | flops | bytes accessed | tf_op | source)
XLA Modules:
  0.0 263.2 jit_solution(11513565188425130312)
XLA Ops:
  0.6 1.3 reshape.66.qkv_b
  1.9 239.6 %step.1 = (bf16[256,1024]{1,0:T(8,128)(2,1)}, f32[256,1024]{1,0:T(8,128)}, f32[16,1024]{1,0:T(8,128)}, bf16[1024,1536]{1,0:T(8,128)(2,1)}, bf16[512,1024]{1,0:T(...) custom-call(bf16[256,1024]{1,0:T(8,128)(2,1)} %hid.1, bf16[256,1024]{1,0:T(8,128)(2,1)} %cot.1, ...), custom_call_target="tpu_custom_call" | custom-call | tf_op jit(solution)/shard_map/step/pallas_call | solution.py:821
  241.5 1.6 broadcast_select_fusion
  243.2 0.0 copy-start.5
  243.2 0.6 pad_maximum_fusion
  243.8 0.6 pad_maximum_fusion.1
  244.4 0.0 copy-start
  244.4 6.8 %convert_element_type.14 = f32[1024,2048]{1,0:T(8,128)} convert(bf16[1024,2048]{1,0:T(8,128)(2,1)} %get-tuple-element.26) | non-fusion elementwise | flops 2097152 | bytes 12582912 | tf_op jit(solution)/shard_map/convert_element_type | solution.py:843
  251.2 0.0 copy-done
  251.2 0.0 copy-start.1
  251.2 4.4 %convert_element_type.15 = f32[2048,1024]{1,0:T(8,128)} convert(bf16[2048,1024]{1,0:T(8,128)(2,1)S(1)} %copy-done) | non-fusion elementwise | flops 2097152 | bytes 12582912 | tf_op jit(solution)/shard_map/convert_element_type | solution.py:843
  255.6 0.0 copy-done.1
  255.6 0.0 copy-start.2
  255.7 0.0 copy-start.4
  255.7 3.6 %convert_element_type.12 = f32[1024,1536]{1,0:T(8,128)} convert(bf16[1024,1536]{1,0:T(8,128)(2,1)S(1)} %copy-done.1) | non-fusion elementwise | flops 1572864 | bytes 9437184 | tf_op jit(solution)/shard_map/convert_element_type | solution.py:843
  259.2 0.0 copy-start.3
  259.2 0.0 copy-done.2
  259.2 1.6 convert_element_type.13
  260.8 0.0 copy-done.5
  260.8 0.6 copy.32
  261.4 0.0 copy-done.4
  261.4 0.8 copy.33
  262.2 0.0 copy-done.3
  262.2 1.0 copy.34
  (1 shorter events, 0.0 us)
Async XLA Ops:
  243.2 17.6 %copy-start.5 = (f32[1,1024]{1,0:T(1,128)}, f32[1,1024]{1,0:T(1,128)S(1)}, u32[]{:S(2)}) copy-start(f32[1,1024]{1,0:T(1,128)S(1)} %get-tuple-element.31) | copy-start | bytes 12292
  244.4 6.8 %copy-start = (bf16[2048,1024]{1,0:T(8,128)(2,1)S(1)}, bf16[2048,1024]{1,0:T(8,128)(2,1)}, u32[]{:S(2)}) copy-start(bf16[2048,1024]{1,0:T(8,128)(2,1)} %get-tuple-element.27) | copy-start | bytes 12582916
  251.2 4.4 %copy-start.1 = (bf16[1024,1536]{1,0:T(8,128)(2,1)S(1)}, bf16[1024,1536]{1,0:T(8,128)(2,1)}, u32[]{:S(2)}) copy-start(bf16[1024,1536]{1,0:T(8,128)(2,1)} %get-tuple-element.24) | copy-start | bytes 9437188
  255.6 3.6 %copy-start.2 = (bf16[512,1024]{1,0:T(8,128)(2,1)S(1)}, bf16[512,1024]{1,0:T(8,128)(2,1)}, u32[]{:S(2)}) copy-start(bf16[512,1024]{1,0:T(8,128)(2,1)} %get-tuple-element.25) | copy-start | bytes 3145732
  255.7 5.7 %copy-start.4 = (bf16[256,1024]{1,0:T(8,128)(2,1)S(1)}, bf16[256,1024]{1,0:T(8,128)(2,1)}, u32[]{:S(2)}) copy-start(bf16[256,1024]{1,0:T(8,128)(2,1)} %get-tuple-element.81) | copy-start | bytes 1572868
  259.2 3.0 %copy-start.3 = (f32[256,1024]{1,0:T(8,128)S(1)}, f32[256,1024]{1,0:T(8,128)}, u32[]{:S(2)}) copy-start(f32[256,1024]{1,0:T(8,128)} %get-tuple-element.82) | copy-start | bytes 3145732

commit v3 on v2

--- a/solution.py
+++ b/solution.py
@@ -63,6 +63,10 @@
         pl.when(when)(action)
 
 
+def row_of(vector):
+    return vector.reshape(1, vector.shape[0])
+
+
 def at(start, size):
     return pl.ds(pl.multiple_of(start, size), size)
 
@@ -75,7 +79,7 @@
     sizes,
     hid, cot, wq, wu, wd, wn, seg, gain1, bias1, gain2, bias2, qkv_b, up_b, dense_b, down_b,
     out, in_grad, small, g_qkv, g_dense, g_up, g_down,
-    X, G, WQ, WU, WD, WN, N, STAT, QKV, ATT, HID, SLOPE, DUP, DAT, OUTP, OZ1, OZ, OY, DZ1, DZ,
+    X, G, WQ, WU, WD, WN, N, STAT, QKV, ATT, HID, SLOPE, DUP, DAT, OUTP, OZ1, OZ2, OZ3, OY, DZ1, DZ, COT,
     S_dn, S_de, S_up, S_qk, R_dn, R_de, V_dn, V_de, X_dn, X_de, A_de, TMP, NV, COS, SIN, NSUM, SMO, SMR, NZ, NQ, BQ, BS, BR,
     send_sem, recv_sem, local_sem, credit,
 ):
@@ -113,6 +117,7 @@
         local.append(copy)
         return copy
 
+    fetch_c = fetch(cot, COT)
     fetch_x = fetch(hid, X.at[at(c * blk, blk), own])
     fetch_g = fetch(cot, G.at[at(c * blk, blk), own])
     fetch_u = fetch(wu.at[:, at(r * units, units)], WU.at[own, :])
@@ -172,7 +177,9 @@
     chain_send("x", 1, X, own, hid)
     copies.start("xy0", hid, X.at[rows(c), other], y_dev)
     for j, vector in enumerate((gain1, bias1, gain2, bias2)):
-        copies.start(f"nv{j}", vector, NV.at[pl.ds(j, 1), other], y_dev)
+        NV[j : j + 1, own] = row_of(vector[...])
+    NV[4:8, own] = jnp.zeros((4, wid), F32)
+    copies.start("nv", NV.at[:, own], NV.at[:, other], y_dev)
     wu_on, wu_far, wu_done = weight(
         "wu", lambda rs: wu.at[rs, at((1 - r) * units, units)], WU, wid, wid // 4, everything, True
     )
@@ -180,8 +187,6 @@
     seg_row = seg[...].astype(F32)
     seg_col = jnp.transpose(jnp.broadcast_to(seg_row, (128, rows_all)))
     STAT[:, 3:4] = seg_col[:, 0:1]
-    for j, vector in enumerate((gain1, bias1, gain2, bias2)):
-        NV[j : j + 1, own] = vector[...]
 
     def table(i):
         block = at(i * blk, blk)
@@ -230,7 +235,7 @@
     def up_block(b):
         def part(j):
             cs = at(j * TILE, TILE)
-            bias = up_b[:, at(r * units + j * TILE, TILE)]
+            bias = row_of(up_b[at(r * units + j * TILE, TILE)])
             up = dot(N[rows(b), :], WU[:, cs], NN) + bias
             cdf = 0.5 * (1.0 + lax.erf(up * (1.0 / math.sqrt(2.0))))
             HID[rows(b), cs] = (up * cdf).astype(BF16)
@@ -240,6 +245,7 @@
 
         tiles(units // TILE, part)
 
+    fetch_c.wait()
     fetch_x.wait()
     fetch_g.wait()
     chain_wait("x", 1)
@@ -250,8 +256,7 @@
     chain_send("x", 3, X, own)
     row_send("xy2", 2)
     chain_send("g", 1, G, own, cot)
-    for j in range(4):
-        copies.came(f"nv{j}")
+    copies.came("nv")
     copies.came("xy0")
     norm_block(col_of[0])
     chain_wait("x", 3)
@@ -264,8 +269,8 @@
     def rows_of(ref, start, rs):
         return ref.at[at(start + rs.start, rs.size), :]
 
-    wn_on, wn_far, wn_done = weight(
-        "wn", lambda rs: rows_of(wn, (1 - r) * units, rs), WN, 0, units // 4, other, True
+    wn_on, _, wn_done = weight(
+        "wn", lambda rs: rows_of(wn, (1 - r) * units, rs), WN, 0, units // 2, other, False
     )
     wd_on, _, wd_done = weight(
         "wd", lambda rs: rows_of(wd, (1 - r) * HD, rs), WD, 0, HD // 2, other, False
@@ -404,7 +409,7 @@
     def qkv_block(i):
         block = at(i * blk, blk)
         for j in range(3):
-            bias = qkv_b[:, at(r * heads + j * HD, HD)]
+            bias = row_of(qkv_b[at(r * heads + j * HD, HD)])
             value = dot(OUTP[block, :], WQ[:, j * HD : (j + 1) * HD], NN) + bias
             if j < 2:
                 value = rotate(value, block, 1.0)
@@ -448,28 +453,22 @@
 
         tiles(wid // TILE, part)
 
-    tiles(cols, lambda b: branch_block(b, 0))
-    wn_on()
+    branch_block(col_of[2], 0)
+    copies.start("oa2", OUTP.at[rows(col_of[2]), own], OZ2.at[:, own], {"col": col_of[2]})
     out_keep("de0", 0, ATT, att_keep, S_de.at[0])
+    copies.start("de0x", S_de.at[0], X_de, x_dev)
+    for s in (3, 1, 0):
+        branch_block(col_of[s], 0)
 
     chain_wait("h", 3)
     out_grad("dn1", 1, HID, hid_keep, hid_send, DUP.at[pl.ds(uh, uh), :], S_dn.at[1])
     out_grad("de1", 1, ATT, att_keep, att_send, A_de.at[1], S_de.at[1])
-    wd_on()
     out_keep("dn1", 1, HID, hid_keep, S_dn.at[1])
     cross("dn1", S_dn.at[1], uh, V_dn)
     out_keep("de1", 1, ATT, att_keep, S_de.at[1])
     cross("de1", S_de.at[1], dh, V_de)
-    copies.start("de0x", S_de.at[0], X_de, x_dev)
-    wd_done()
-    wn_far()
+    wn_on()
     wn_done()
-    for s in (2, 3):
-        branch_block(col_of[s], 1)
-        copies.start(f"oy{s}", OUTP.at[rows(col_of[s]), other], OY.at[s - 1], y_dev)
-    branch_block(col_of[1], 1)
-    copies.start("oz1", OUTP.at[rows(col_of[1]), :], OZ1, {"col": col_of[1]})
-    branch_block(col_of[0], 1)
 
     copies.sent("dn0a", "dn1a")
 
@@ -508,6 +507,8 @@
     in_give(
         "up", DUP, give_u, uh, [SLOPE.at[:, pl.ds(0, uh)], SLOPE.at[:, pl.ds(uh, uh)]], S_up
     )
+    wd_on()
+    wd_done()
     for i in range(cols):
         mine = slice(i * blk, (i + 1) * blk)
         DAT[mine, :] = dot(G[mine, :], WD[...], NT).astype(BF16)
@@ -521,32 +522,37 @@
     X_qk = WN.at[:, pl.ds(0, hh)]
     V_qk, R_qk = WN.at[low, pl.ds(hh, hh)], WN.at[high, pl.ds(hh, hh)]
 
+    crossed("dn1", R_dn)
     in_keep("up", 1, DUP, keep_u, S_up)
     pl.semaphore_wait(credit.at[0], 1)
     cross("up1", S_up.at[1], wid, V_up)
     in_keep("up", 0, DUP, keep_u, S_up)
     copies.start("up0x", S_up.at[0], X_up, x_dev)
 
-    crossed("dn1", R_dn)
+    branch_block(col_of[3], 1)
+    copies.start("oy3", OUTP.at[rows(col_of[3]), other], OY.at[1], y_dev)
+    branch_block(col_of[2], 1)
+    copies.start("ob2", OUTP.at[rows(col_of[2]), other], OZ2.at[:, other], {"col": col_of[2]})
+    branch_block(col_of[1], 1)
+    copies.start("oz1", OUTP.at[rows(col_of[1]), :], OZ1, {"col": col_of[1]})
+    branch_block(col_of[0], 1)
     crossed("de1", R_de)
-    copies.sent("wnx", "wnc", "wnf")
+    copies.sent("wnc")
     pl.semaphore_signal(credit.at[2], inc=1, device_id=x_dev, device_id_type=MESH)
     pl.semaphore_signal(credit.at[3], inc=1, device_id=y_dev, device_id_type=MESH)
     pl.semaphore_signal(credit.at[4], inc=1, device_id=y_dev, device_id_type=MESH)
 
-    def out_block(s):
-        b = col_of[s]
-        copies.came(f"oy{s}")
+    def out_block():
+        b = col_of[3]
+        copies.came("oy3")
 
         def part(i):
             rs = at(b * blk + i * sub, sub)
-            came = OY[s - 1, at(i * sub, sub), :]
+            came = OY[1, at(i * sub, sub), :]
             OUTP[rs, own] = (OUTP[rs, own].astype(F32) + came.astype(F32)).astype(BF16)
 
         tiles(blk // sub, part)
-        copies.start(f"oz{s}", OUTP.at[rows(b), own], OZ.at[s - 2], {"col": b})
-
-    out_block(2)
+        copies.start("oz3", OUTP.at[rows(b), own], OZ3, {"col": b})
 
     def again(i):
         rs = at(i * sub, sub)
@@ -554,7 +560,6 @@
         N[rs, :] = (normal * NV[0:1, :] + NV[1:2, :]).astype(BF16)
 
     tiles(rows_all // sub, again)
-    out_block(3)
     TMP[...] = jnp.zeros_like(TMP)
     for i in range(cols):
         mine, span, low = key_range(i)
@@ -644,6 +649,7 @@
         norm_back(col_of[s])
         copies.start(f"ey{s}", N.at[rows(col_of[s]), other], EY[s - 1], y_dev)
         if s == 2:
+            out_block()
             spread_out("dn1", R_dn, g_down, down_at(1 - r, hi))
         else:
             spread_out("de1", R_de, g_dense, dense_at(1 - r, hi))
@@ -656,23 +662,28 @@
     def mine_at(i):
         return at(c * blk + i * sub, sub)
 
-    def row_rest(buf, came, landing, name):
-        copies.came(f"{name}z1")
+    def row_rest(buf, names, whole, landing, name):
+        for arrival in names:
+            copies.came(arrival)
 
         def part(i):
             rs = at(i * sub, sub)
-            total = buf[mine_at(i), other].astype(F32) + came[rs, other].astype(F32)
+            total = buf[mine_at(i), other].astype(F32)
+            for ref in whole:
+                total = total + ref[rs, other].astype(F32)
             buf[mine_at(i), other] = total.astype(BF16)
 
         tiles(blk // sub, part)
-        copies.start(f"{name}y0", buf.at[rows(c), other], landing, y_dev)
-
-    def total_of(i, buf, near, far_ones, from_row):
+        copies.start(name, buf.at[rows(c), other], landing, y_dev)
+
+    def total_of(i, buf, whole, parts):
         rs = at(i * sub, sub)
-        total = buf[mine_at(i), own].astype(F32) + near[rs, own].astype(F32)
-        for ref in far_ones:
+        total = buf[mine_at(i), own].astype(F32)
+        for ref in whole:
+            total = total + ref[rs, own].astype(F32)
+        for ref in parts:
             total = total + ref[rs, :].astype(F32)
-        return total + from_row[rs, :].astype(F32)
+        return total
 
     def x_block(s):
         b = col_of[s]
@@ -686,7 +697,7 @@
         tiles(blk // sub, part)
         copies.start(f"ez{s}", N.at[rows(b), own], DZ.at[s - 2], {"col": b})
 
-    row_rest(OUTP, OZ1, OY.at[0], "o")
+    row_rest(OUTP, ("oz1", "oa2", "ob2"), (OZ1, OZ2), OY.at[0], "oy0")
     spread_out("up1", R_up, g_up, up_at(1 - r, hi))
     finish("dn0", S_dn.at[0], X_dn, g_down, down_at(r))
     finish("de0", S_de.at[0], X_de, g_dense, dense_at(r))
@@ -698,7 +709,7 @@
     for s in (1, 2, 3):
         copies.start(f"sz{s}", NZ.at[c], NZ.at[c], {"col": col_of[s]})
     x_block(3)
-    row_rest(N, DZ1, EY[0], "e")
+    row_rest(N, ("ez1",), (DZ1,), EY[0], "ey0")
     BS[...] = gathered_dp("b", BQ)
     copies.start("by", BS, BR, y_dev)
     finish("qk0", S_qk.at[0], X_qk, g_qkv, qkv_at(r))
@@ -709,13 +720,13 @@
     pass_quarter("dn1", g_down, down_at(1 - r, 1 - hi))
     pass_quarter("de1", g_dense, dense_at(1 - r, 1 - hi))
     spread_out("qk1", R_qk, g_qkv, qkv_at(1 - r, hi))
-    for name in ("oz2", "oz3", "oy0"):
+    for name in ("oz3", "oy0"):
         copies.came(name)
 
     def out_last(i):
-        total = total_of(i, OUTP, OZ1, [OZ.at[0], OZ.at[1]], OY.at[0])
+        total = total_of(i, OUTP, (OZ1, OZ2), (OZ3, OY.at[0]))
         total = total + X[mine_at(i), own].astype(F32)
-        out[at(i * sub, sub), :] = (total + (dense_b[...] + down_b[...])).astype(BF16)
+        out[at(i * sub, sub), :] = (total + row_of(dense_b[...] + down_b[...])).astype(BF16)
 
     tiles(blk // sub, out_last)
     pass_quarter("up1", g_up, up_at(1 - r, 1 - hi))
@@ -727,8 +738,8 @@
         copies.came(name)
 
     def x_last(i):
-        total = total_of(i, N, DZ1, [DZ.at[0], DZ.at[1]], EY[0])
-        in_grad[at(i * sub, sub), :] = cot[at(i * sub, sub), :].astype(F32) + total
+        total = total_of(i, N, (DZ1,), (DZ.at[0], DZ.at[1], EY[0]))
+        in_grad[at(i * sub, sub), :] = COT[at(i * sub, sub), :].astype(F32) + total
 
     tiles(blk // sub, x_last)
     pass_quarter("qk1", g_qkv, qkv_at(1 - r, 1 - hi))
@@ -737,7 +748,7 @@
     for name in ("dn1", "de1", "up1", "qk1"):
         copies.came(f"{name}t")
         copies.came(f"{name}f")
-    for copy in local[6:]:
+    for copy in local[7:]:
         copy.wait()
     copies.sent_all()
 
@@ -756,8 +767,8 @@
             V(shape, BF16)
             for shape in (
                 (tokens, heads), (tokens, HD), (tokens, units), (tokens, units), (tokens, units),
-                (tokens, HD), (tokens, width), (blk, width), (2, blk, wid), (3, blk, wid),
-                (blk, width), (2, blk, wid),
+                (tokens, HD), (tokens, width), (blk, width), (blk, width), (blk, wid),
+                (2, blk, wid), (blk, width), (2, blk, wid), (blk, wid),
                 (2, units // 2, wid), (2, HD // 2, wid), (2, wid, units // 2), (2, wid, heads // 2),
                 (units // 4, wid), (HD // 4, wid), (units // 4, wid), (HD // 4, wid),
                 (units // 2, wid), (HD // 2, wid), (2, HD // 2, wid),
@@ -784,6 +795,26 @@
     )
 
 
+def widen_kernel(*refs):
+    given, results = refs[:7], refs[7:]
+    small = given[6]
+    for source, target in zip(given[:6], results[:6]):
+        target[...] = source[...].astype(target.dtype)
+
+    @pl.when(pl.program_id(0) == 0)
+    def _():
+        gain1, bias1, gain2, bias2, qkv_sum, dense_sum, up_sum, down_sum = results[6:]
+        for j, ref in enumerate((gain1, bias1, gain2, bias2)):
+            ref[...] = small[4 + j]
+        dense_sum[...] = small[2]
+        down_sum[...] = small[2]
+        r = lax.axis_index("row")
+        for ref, index in ((up_sum, 0), (qkv_sum, 1)):
+            n = ref.shape[0] // 2
+            ref[at(r * n, n)] = small[index, 0:n]
+            ref[at((1 - r) * n, n)] = small[8 + index, 0:n]
+
+
 def swap(value, axis, mask):
     size = lax.axis_size(axis)
     return lax.ppermute(value, axis, [(i, i ^ mask) for i in range(size)])
@@ -809,12 +840,9 @@
     blk, wid = hidden_in.shape
     cols = lax.axis_size("col")
     heads, units = qkv_weight.shape[1] // 2, up_weight.shape[1] // 2
-    vectors = [
-        v.reshape(1, -1)
-        for v in (
-            norm1_gain, norm1_bias, norm2_gain, norm2_bias, qkv_bias, up_bias, dense_bias, down_bias,
-        )
-    ]
+    vectors = (
+        norm1_gain, norm1_bias, norm2_gain, norm2_bias, qkv_bias, up_bias, dense_bias, down_bias,
+    )
     vmem = pl.BlockSpec(memory_space=pltpu.VMEM)
     far = pl.BlockSpec(memory_space=pl.ANY)
     shape = jax.ShapeDtypeStruct
@@ -829,7 +857,7 @@
             shape(up_weight.shape, BF16),
             shape(down_weight.shape, BF16),
         ),
-        in_specs=[vmem, vmem] + [far] * 4 + [vmem] * 9,
+        in_specs=[far] * 6 + [vmem] * 9,
         out_specs=(vmem,) * 3 + (far,) * 4,
         scratch_shapes=scratch(blk, wid, cols, units, heads),
         compiler_params=pltpu.CompilerParams(
@@ -840,35 +868,53 @@
         hidden_in, cotangent, qkv_weight, up_weight, dense_weight, down_weight, segment, *vectors
     )
 
-    grads = [g.astype(F32) for g in (g_qkv, g_dense, g_up, g_down)]
+    grads = (g_qkv, g_dense, g_up, g_down)
     mask = 4
     while mask < lax.axis_size("dp"):
-        grads = [g + swap(g.astype(BF16), "dp", mask).astype(F32) for g in grads]
+        grads = tuple(
+            (g.astype(F32) + swap(g, "dp", mask).astype(F32)).astype(BF16) for g in grads
+        )
         small = small + swap(small, "dp", mask)
         mask *= 2
-    row = lax.axis_index("row")
-
-    def both(index):
-        first, second = small[index], small[8 + index]
-        return jnp.where(row == 0, first, second), jnp.where(row == 0, second, first)
-
-    qkv_bias_grad = jnp.concatenate([part[:heads] for part in both(1)])
-    up_bias_grad = jnp.concatenate(both(0))
+    steps = 4
+
+    def cut(array):
+        rows, columns = array.shape
+        return pl.BlockSpec((rows // steps, columns), lambda i: (i, 0))
+
+    def whole(n):
+        return pl.BlockSpec((n,), lambda i: (0,))
+
+    lengths = [wid] * 4 + [2 * heads, wid, 2 * units, wid]
+    widened = pl.pallas_call(
+        widen_kernel,
+        grid=(steps,),
+        out_shape=[shape(out.shape, BF16), shape(in_grad.shape, F32)]
+        + [shape(g.shape, F32) for g in grads]
+        + [shape((n,), F32) for n in lengths],
+        in_specs=[cut(out), cut(in_grad)]
+        + [cut(g) for g in grads]
+        + [pl.BlockSpec(small.shape, lambda i: (0, 0))],
+        out_specs=[cut(out), cut(in_grad)] + [cut(g) for g in grads] + [whole(n) for n in lengths],
+        compiler_params=pltpu.CompilerParams(vmem_limit_bytes=60 << 20),
+        name="widen",
+    )(out, in_grad, *grads, small)
+    out, in_grad, d_qkv, d_dense, d_up, d_down, *sums = widened
     return (
         out,
         in_grad,
-        small[4],
-        small[5],
-        small[6],
-        small[7],
-        grads[0],
-        qkv_bias_grad,
-        grads[1],
-        small[2],
-        grads[2],
-        up_bias_grad,
-        grads[3],
-        small[2],
+        sums[0],
+        sums[1],
+        sums[2],
+        sums[3],
+        d_qkv,
+        sums[4],
+        d_dense,
+        sums[5],
+        d_up,
+        sums[6],
+        d_down,
+        sums[7],
     )
 
 

time: 265 us -> 255 us (0.962)
  other arithmetic: 19.3 us -> 0 us
  Pallas kernels: 240 us -> 253 us
  local copies, waits for them, and re-layouts: 3.67 us -> 0 us
    convert_element_type x4 -> x0, other arithmetic: 16.4 us -> none  [shards(): grads = [g.astype(F32) for g in (g_qkv, g_dense, g_up, g_down)]]
    pallas_call x0 -> x1, Pallas kernels: none -> 13.9 us  [shards(): pl.pallas_call(widen_kernel, grid=(steps,), out_shape=[shape(out.shape, B...]
where the time goes in v3:
time: 255 us; the launch traced here: 254 us
  Pallas kernels  253 us (99%)
    pallas_call x1, Pallas kernels, shards(): pl.pallas_call(functools.partial(step_kernel, (blk, wid, cols)), out_shap...  239 us
    pallas_call x1, Pallas kernels, shards(): pl.pallas_call(widen_kernel, grid=(steps,), out_shape=[shape(out.shape, B...  13.9 us

profile of v3, /device:TPU:9, one launch (start us, length us, event | category | flops | bytes accessed | tf_op | source)
XLA Modules:
  0.0 253.9 jit_solution(15891067828586006498)
XLA Ops:
  0.7 239.2 %step.1 = (bf16[256,1024]{1,0:T(8,128)(2,1)}, f32[256,1024]{1,0:T(8,128)}, f32[16,1024]{1,0:T(8,128)}, bf16[1024,1536]{1,0:T(8,128)(2,1)}, bf16[512,1024]{1,0:T(...) custom-call(bf16[256,1024]{1,0:T(8,128)(2,1)} %hid.1, bf16[256,1024]{1,0:T(8,128)(2,1)} %cot.1, ...), custom_call_target="tpu_custom_call" | custom-call | tf_op jit(solution)/shard_map/step/pallas_call | solution.py:849
  239.8 13.9 %widen.1 = (bf16[256,1024]{1,0:T(8,128)(2,1)}, f32[256,1024]{1,0:T(8,128)}, f32[1024,1536]{1,0:T(8,128)}, f32[512,1024]{1,0:T(8,128)}, f32[1024,2048]{1,0:T(8,12...) custom-call(bf16[256,1024]{1,0:T(8,128)(2,1)} %get-tuple-element.35., ...), custom_call_target="tpu_custom_call" | custom-call | tf_op jit(solution)/shard_map/widen/pallas_call | solution.py:889

commit v4 on v3

--- a/solution.py
+++ b/solution.py
@@ -105,9 +105,15 @@
     copies = Copies(send_sem, recv_sem)
 
     barrier = pltpu.get_barrier_semaphore()
-    friends = [core_dev, x_dev, far_dev, y_dev] + [{"col": col_of[s]} for s in (1, 2, 3)]
-    for device in friends:
+    for device in (core_dev, x_dev, y_dev):
         pl.semaphore_signal(barrier, inc=1, device_id=device, device_id_type=MESH)
+    for move, inside in ((1, c < cols - 1), (-1, c >= 1)):
+
+        @pl.when(inside)
+        def _():
+            pl.semaphore_signal(
+                barrier, inc=1, device_id={"col": c + move}, device_id_type=MESH
+            )
 
     local = []
 
@@ -124,7 +130,9 @@
     fetch_q = fetch(wq.at[:, at(r * heads, heads)], WQ.at[own, :])
     fetch_n = fetch(wn.at[at(r * units, units), :], WN.at[:, own])
     fetch_d = fetch(wd.at[at(r * HD, HD), :], WD.at[:, own])
-    pl.semaphore_wait(barrier, len(friends))
+    pl.semaphore_wait(
+        barrier, 3 + (c < cols - 1).astype(jnp.int32) + (c >= 1).astype(jnp.int32)
+    )
 
     def rows(b):
         return at(b * blk, blk)
@@ -251,11 +259,11 @@
     chain_wait("x", 1)
     chain_send("x", 2, X, own)
     row_send("xy1", 1)
-    wu_on()
     chain_wait("x", 2)
     chain_send("x", 3, X, own)
     row_send("xy2", 2)
     chain_send("g", 1, G, own, cot)
+    wu_on()
     copies.came("nv")
     copies.came("xy0")
     norm_block(col_of[0])
@@ -454,21 +462,23 @@
         tiles(wid // TILE, part)
 
     branch_block(col_of[2], 0)
-    copies.start("oa2", OUTP.at[rows(col_of[2]), own], OZ2.at[:, own], {"col": col_of[2]})
     out_keep("de0", 0, ATT, att_keep, S_de.at[0])
     copies.start("de0x", S_de.at[0], X_de, x_dev)
     for s in (3, 1, 0):
         branch_block(col_of[s], 0)
 
     chain_wait("h", 3)
+    copies.start("oa1", OUTP.at[rows(col_of[1]), own], OZ1.at[:, own], {"col": col_of[1]})
     out_grad("dn1", 1, HID, hid_keep, hid_send, DUP.at[pl.ds(uh, uh), :], S_dn.at[1])
     out_grad("de1", 1, ATT, att_keep, att_send, A_de.at[1], S_de.at[1])
+    wn_on()
     out_keep("dn1", 1, HID, hid_keep, S_dn.at[1])
     cross("dn1", S_dn.at[1], uh, V_dn)
     out_keep("de1", 1, ATT, att_keep, S_de.at[1])
     cross("de1", S_de.at[1], dh, V_de)
-    wn_on()
     wn_done()
+    copies.start("oa2", OUTP.at[rows(col_of[2]), own], OZ2.at[:, own], {"col": col_of[2]})
+    wd_on()
 
     copies.sent("dn0a", "dn1a")
 
@@ -483,16 +493,14 @@
     keep_u, give_u = at(k * uh, uh), at((1 - k) * uh, uh)
     keep_h, give_h = at(k * hh, hh), at((1 - k) * hh, hh)
 
-    def in_give(name, right_ref, give, n, staged, landing):
-        for side in (0, 1):
-
-            def part(i):
-                rs = at(i * TILE, TILE)
-                lefts = N[:, at(side * wid + i * TILE, TILE)]
-                staged[side][rs, :] = dot(lefts, right_ref[:, give], TN).astype(BF16)
-
-            tiles(wid // TILE, part)
-            copies.start(f"{name}{side}a", staged[side], landing.at[side], core_dev)
+    def in_give(name, side, right_ref, give, staged, landing):
+        def part(i):
+            rs = at(i * TILE, TILE)
+            lefts = N[:, at(side * wid + i * TILE, TILE)]
+            staged[rs, :] = dot(lefts, right_ref[:, give], TN).astype(BF16)
+
+        tiles(wid // TILE, part)
+        copies.start(f"{name}{side}a", staged, landing.at[side], core_dev)
 
     def in_keep(name, side, right_ref, keep, landing):
         copies.came(f"{name}{side}a")
@@ -504,11 +512,10 @@
 
         tiles(wid // TILE, part)
 
-    in_give(
-        "up", DUP, give_u, uh, [SLOPE.at[:, pl.ds(0, uh)], SLOPE.at[:, pl.ds(uh, uh)]], S_up
-    )
-    wd_on()
     wd_done()
+    branch_block(col_of[3], 1)
+    copies.start("oy3", OUTP.at[rows(col_of[3]), other], OY.at[1], y_dev)
+    in_give("up", 1, DUP, give_u, SLOPE.at[:, pl.ds(uh, uh)], S_up)
     for i in range(cols):
         mine = slice(i * blk, (i + 1) * blk)
         DAT[mine, :] = dot(G[mine, :], WD[...], NT).astype(BF16)
@@ -522,19 +529,18 @@
     X_qk = WN.at[:, pl.ds(0, hh)]
     V_qk, R_qk = WN.at[low, pl.ds(hh, hh)], WN.at[high, pl.ds(hh, hh)]
 
-    crossed("dn1", R_dn)
     in_keep("up", 1, DUP, keep_u, S_up)
     pl.semaphore_wait(credit.at[0], 1)
     cross("up1", S_up.at[1], wid, V_up)
+    crossed("dn1", R_dn)
+    in_give("up", 0, DUP, give_u, SLOPE.at[:, pl.ds(0, uh)], S_up)
+    branch_block(col_of[2], 1)
+    copies.start("ob2", OUTP.at[rows(col_of[2]), other], OZ2.at[:, other], {"col": col_of[2]})
     in_keep("up", 0, DUP, keep_u, S_up)
     copies.start("up0x", S_up.at[0], X_up, x_dev)
 
-    branch_block(col_of[3], 1)
-    copies.start("oy3", OUTP.at[rows(col_of[3]), other], OY.at[1], y_dev)
-    branch_block(col_of[2], 1)
-    copies.start("ob2", OUTP.at[rows(col_of[2]), other], OZ2.at[:, other], {"col": col_of[2]})
     branch_block(col_of[1], 1)
-    copies.start("oz1", OUTP.at[rows(col_of[1]), :], OZ1, {"col": col_of[1]})
+    copies.start("ob1", OUTP.at[rows(col_of[1]), other], OZ1.at[:, other], {"col": col_of[1]})
     branch_block(col_of[0], 1)
     crossed("de1", R_de)
     copies.sent("wnc")
@@ -583,9 +589,8 @@
         QKV[mine, 2 * HD :] = TMP[:, vs].astype(BF16)
 
     copies.sent("up0a", "up1a")
-    in_give(
-        "qk", QKV, give_h, hh, [SLOPE.at[:, pl.ds(0, hh)], SLOPE.at[:, pl.ds(hh, hh)]], S_qk
-    )
+    in_give("qk", 1, QKV, give_h, SLOPE.at[:, pl.ds(hh, hh)], S_qk)
+    in_give("qk", 0, QKV, give_h, SLOPE.at[:, pl.ds(0, hh)], S_qk)
     pl.semaphore_wait(credit.at[1], 1)
     crossed("up1", R_up)
     in_keep("qk", 1, QKV, keep_h, S_qk)
@@ -654,7 +659,9 @@
         else:
             spread_out("de1", R_de, g_dense, dense_at(1 - r, hi))
     norm_back(col_of[1])
-    copies.start("ez1", N.at[rows(col_of[1]), :], DZ1, {"col": col_of[1]})
+    copies.start(
+        "ezb", N.at[rows(col_of[1]), other], DZ1.at[:, other], {"col": col_of[1]}
+    )
     norm_back(col_of[0])
     SMO[0:4, :] = NSUM[0:4, other]
     copies.start("sy", SMO, SMR, y_dev)
@@ -685,6 +692,8 @@
             total = total + ref[rs, :].astype(F32)
         return total
 
+    at_end, between = lax.rem(c, 3) == 0, lax.rem(c, 3) != 0
+
     def x_block(s):
         b = col_of[s]
         copies.came(f"ey{s}")
@@ -695,9 +704,26 @@
             N[rs, own] = (N[rs, own].astype(F32) + came.astype(F32)).astype(BF16)
 
         tiles(blk // sub, part)
-        copies.start(f"ez{s}", N.at[rows(b), own], DZ.at[s - 2], {"col": b})
-
-    row_rest(OUTP, ("oz1", "oa2", "ob2"), (OZ1, OZ2), OY.at[0], "oy0")
+        copies.start(
+            f"ea{s}", N.at[rows(b), own], DZ.at[s - 2], {"col": col_of[1]}, at_end
+        )
+
+    def x_pass(s):
+        b = col_of[s]
+        copies.came(f"ea{5 - s}", between)
+
+        @pl.when(between)
+        def _():
+            def part(i):
+                rs = at(b * blk + i * sub, sub)
+                came = DZ[3 - s, at(i * sub, sub), :]
+                N[rs, own] = (N[rs, own].astype(F32) + came.astype(F32)).astype(BF16)
+
+            tiles(blk // sub, part)
+
+        copies.start(f"eb{s}", N.at[rows(b), own], DZ.at[2], {"col": b}, between)
+
+    row_rest(OUTP, ("oa1", "oa2", "ob1", "ob2"), (OZ1, OZ2), OY.at[0], "oy0")
     spread_out("up1", R_up, g_up, up_at(1 - r, hi))
     finish("dn0", S_dn.at[0], X_dn, g_down, down_at(r))
     finish("de0", S_de.at[0], X_de, g_dense, dense_at(r))
@@ -709,15 +735,18 @@
     for s in (1, 2, 3):
         copies.start(f"sz{s}", NZ.at[c], NZ.at[c], {"col": col_of[s]})
     x_block(3)
-    row_rest(N, ("ez1",), (DZ1,), EY[0], "ey0")
+    copies.start("eza", N.at[rows(col_of[1]), own], DZ1.at[:, own], {"col": col_of[1]})
     BS[...] = gathered_dp("b", BQ)
     copies.start("by", BS, BR, y_dev)
+    row_rest(N, ("ezb",), (DZ1,), EY[0], "ey0")
+    x_pass(3)
     finish("qk0", S_qk.at[0], X_qk, g_qkv, qkv_at(r))
+    pass_quarter("dn1", g_down, down_at(1 - r, 1 - hi))
+    x_pass(2)
     for s in (1, 2, 3):
         copies.came(f"sz{s}")
     NQ[q] = NZ[0] + NZ[1] + NZ[2] + NZ[3]
     gather_dp("n", NQ)
-    pass_quarter("dn1", g_down, down_at(1 - r, 1 - hi))
     pass_quarter("de1", g_dense, dense_at(1 - r, 1 - hi))
     spread_out("qk1", R_qk, g_qkv, qkv_at(1 - r, hi))
     for name in ("oz3", "oy0"):
@@ -734,11 +763,13 @@
     small[0:8, :] = BS[...]
     small[8:16, :] = BR[...]
     small[4:8, :] = gathered_dp("n", NQ)[0:4]
-    for name in ("ez2", "ez3", "ey0"):
-        copies.came(name)
+    copies.came("eza")
+    copies.came("eb2", at_end)
+    copies.came("eb3", between)
+    copies.came("ey0")
 
     def x_last(i):
-        total = total_of(i, N, (DZ1,), (DZ.at[0], DZ.at[1], EY[0]))
+        total = total_of(i, N, (DZ1,), (DZ.at[2], EY[0]))
         in_grad[at(i * sub, sub), :] = COT[at(i * sub, sub), :].astype(F32) + total
 
     tiles(blk // sub, x_last)
@@ -768,7 +799,7 @@
             for shape in (
                 (tokens, heads), (tokens, HD), (tokens, units), (tokens, units), (tokens, units),
                 (tokens, HD), (tokens, width), (blk, width), (blk, width), (blk, wid),
-                (2, blk, wid), (blk, width), (2, blk, wid), (blk, wid),
+                (2, blk, wid), (blk, width), (3, blk, wid), (blk, wid),
                 (2, units // 2, wid), (2, HD // 2, wid), (2, wid, units // 2), (2, wid, heads // 2),
                 (units // 4, wid), (HD // 4, wid), (units // 4, wid), (HD // 4, wid),
                 (units // 2, wid), (HD // 2, wid), (2, HD // 2, wid),

time: 255 us -> 250 us (0.980)
  Pallas kernels: 253 us -> 246 us
    pallas_call x1, Pallas kernels: 239 us -> 232 us  [shards(): pl.pallas_call(functools.partial(step_kernel, (blk, wid, cols)), out_shap...]
where the time goes in v4:
time: 250 us; the launch traced here: 247 us
  Pallas kernels  246 us (98%)
    pallas_call x1, Pallas kernels, shards(): pl.pallas_call(functools.partial(step_kernel, (blk, wid, cols)), out_shap...  232 us
    pallas_call x1, Pallas kernels, shards(): pl.pallas_call(widen_kernel, grid=(steps,), out_shape=[shape(out.shape, B...  13.9 us

profile of v4, /device:TPU:9, one launch (start us, length us, event | category | flops | bytes accessed | tf_op | source)
XLA Modules:
  0.0 247.2 jit_solution(3586583449339774165)
XLA Ops:
  0.7 232.5 %step.1 = (bf16[256,1024]{1,0:T(8,128)(2,1)}, f32[256,1024]{1,0:T(8,128)}, f32[16,1024]{1,0:T(8,128)}, bf16[1024,1536]{1,0:T(8,128)(2,1)}, bf16[512,1024]{1,0:T(...) custom-call(bf16[256,1024]{1,0:T(8,128)(2,1)} %hid.1, bf16[256,1024]{1,0:T(8,128)(2,1)} %cot.1, ...), custom_call_target="tpu_custom_call" | custom-call | tf_op jit(solution)/shard_map/step/pallas_call | solution.py:880
  233.1 13.9 %widen.1 = (bf16[256,1024]{1,0:T(8,128)(2,1)}, f32[256,1024]{1,0:T(8,128)}, f32[1024,1536]{1,0:T(8,128)}, f32[512,1024]{1,0:T(8,128)}, f32[1024,2048]{1,0:T(8,12...) custom-call(bf16[256,1024]{1,0:T(8,128)(2,1)} %get-tuple-element.35., ...), custom_call_target="tpu_custom_call" | custom-call | tf_op jit(solution)/shard_map/widen/pallas_call | solution.py:920

commit v5 on v4

--- a/solution.py
+++ b/solution.py
@@ -78,8 +78,8 @@
 def step_kernel(
     sizes,
     hid, cot, wq, wu, wd, wn, seg, gain1, bias1, gain2, bias2, qkv_b, up_b, dense_b, down_b,
-    out, in_grad, small, g_qkv, g_dense, g_up, g_down,
-    X, G, WQ, WU, WD, WN, N, STAT, QKV, ATT, HID, SLOPE, DUP, DAT, OUTP, OZ1, OZ2, OZ3, OY, DZ1, DZ, COT,
+    out_hbm, in_grad_hbm, small_hbm, g_qkv, g_dense, g_up, g_down,
+    out, in_grad, small, X, G, WQ, WU, WD, WN, N, STAT, QKV, ATT, HID, SLOPE, DUP, DAT, OUTP, OZ1, OZ2, OZ3, OY, DZ1, DZ, COT,
     S_dn, S_de, S_up, S_qk, R_dn, R_de, V_dn, V_de, X_dn, X_de, A_de, TMP, NV, COS, SIN, NSUM, SMO, SMR, NZ, NQ, BQ, BS, BR,
     send_sem, recv_sem, local_sem, credit,
 ):
@@ -337,6 +337,26 @@
 
         tiles(wid // TILE, keep_part)
 
+    down_tiles = [slice(i * TILE, (i + 1) * TILE) for i in range(wid // TILE)]
+
+    def down_give(side, staged):
+        for i, cs in enumerate(down_tiles):
+            part = dot(HID[:, hid_send], G[:, side * wid + i * TILE : side * wid + (i + 1) * TILE], TN)
+            staged[:, cs] = part.astype(BF16)
+            copies.start(f"dn{side}a{i}", staged.at[:, cs], S_dn.at[side, :, cs], core_dev)
+
+    def down_keep(side):
+        half_rows = uh // 2
+        give = at((1 - hi) * half_rows, half_rows)
+        for i, cs in enumerate(down_tiles):
+            copies.came(f"dn{side}a{i}")
+            mine = dot(HID[:, hid_keep], G[:, side * wid + i * TILE : side * wid + (i + 1) * TILE], TN)
+            S_dn[side, :, cs] = (mine + S_dn[side, :, cs].astype(F32)).astype(BF16)
+            if side == 0:
+                copies.start(f"dn0x{i}", S_dn.at[0, :, cs], X_dn.at[:, cs], x_dev)
+            else:
+                copies.start(f"dn1x{i}", S_dn.at[1, give, cs], V_dn.at[:, cs], x_dev)
+
     halves = {}
 
     def cross(name, total, n_rows, landing):
@@ -345,9 +365,10 @@
         copies.start(f"{name}x", total.at[give, :], landing, x_dev)
         halves[name] = (total.at[keep, :], landing)
 
-    def crossed(name, target):
+    def crossed(name, target, parts=("",)):
         mine, landing = halves[name]
-        copies.came(f"{name}x")
+        for word in parts:
+            copies.came(f"{name}x{word}")
         n = landing.shape[0]
         step = min(n, 128)
 
@@ -368,8 +389,9 @@
         copies.came(f"{name}g")
         copies.start(f"{name}f", result.at[there], result.at[there], core_dev)
 
-    def finish(name, total, came, result, here):
-        copies.came(f"{name}x")
+    def finish(name, total, came, result, here, parts=("",)):
+        for word in parts:
+            copies.came(f"{name}x{word}")
         n = total.shape[0]
         step = min(n, 128)
 
@@ -404,9 +426,9 @@
         return (taken, at(side * heads + k * hh, hh))
 
     chain_wait("g", 3)
-    out_grad("dn0", 0, HID, hid_keep, hid_send, DUP.at[pl.ds(0, uh), :], S_dn.at[0])
-    out_keep("dn0", 0, HID, hid_keep, S_dn.at[0])
-    copies.start("dn0x", S_dn.at[0], X_dn, x_dev)
+    both_tiles = tuple(range(len(down_tiles)))
+    down_give(0, DUP.at[pl.ds(0, uh), :])
+    down_keep(0)
 
     chain_wait("h", 1)
     chain_send("h", 2, G, other)
@@ -468,19 +490,27 @@
         branch_block(col_of[s], 0)
 
     chain_wait("h", 3)
-    copies.start("oa1", OUTP.at[rows(col_of[1]), own], OZ1.at[:, own], {"col": col_of[1]})
-    out_grad("dn1", 1, HID, hid_keep, hid_send, DUP.at[pl.ds(uh, uh), :], S_dn.at[1])
+    at_end, between = lax.rem(c, 3) == 0, lax.rem(c, 3) != 0
+
+    def own_near(name, when):
+        copies.start(
+            name, OUTP.at[rows(col_of[1]), own], OZ1.at[:, own], {"col": col_of[1]}, when
+        )
+
+    own_near("oa1", at_end)
+    down_give(1, DUP.at[pl.ds(uh, uh), :])
     out_grad("de1", 1, ATT, att_keep, att_send, A_de.at[1], S_de.at[1])
     wn_on()
-    out_keep("dn1", 1, HID, hid_keep, S_dn.at[1])
-    cross("dn1", S_dn.at[1], uh, V_dn)
+    down_keep(1)
+    halves["dn1"] = (S_dn.at[1, at(hi * (uh // 2), uh // 2), :], V_dn)
     out_keep("de1", 1, ATT, att_keep, S_de.at[1])
     cross("de1", S_de.at[1], dh, V_de)
+    own_near("oc1", between)
     wn_done()
     copies.start("oa2", OUTP.at[rows(col_of[2]), own], OZ2.at[:, own], {"col": col_of[2]})
     wd_on()
 
-    copies.sent("dn0a", "dn1a")
+    copies.sent(*[f"dn{side}a{i}" for side in (0, 1) for i in both_tiles])
 
     def up_grad_part(i):
         block = at(i * blk, blk)
@@ -502,15 +532,21 @@
         tiles(wid // TILE, part)
         copies.start(f"{name}{side}a", staged, landing.at[side], core_dev)
 
-    def in_keep(name, side, right_ref, keep, landing):
+    def in_keep(name, side, right_ref, keep, landing, crossing=None):
         copies.came(f"{name}{side}a")
+        n = wid // 2
 
         def part(i):
-            rs = at(i * TILE, TILE)
-            mine = dot(N[:, at(side * wid + i * TILE, TILE)], right_ref[:, keep], TN)
+            rs = at(i * n, n)
+            mine = dot(N[:, at(side * wid + i * n, n)], right_ref[:, keep], TN)
             landing[side, rs, :] = (mine + landing[side, rs, :].astype(F32)).astype(BF16)
 
-        tiles(wid // TILE, part)
+        if crossing is None:
+            tiles(2, part)
+        else:
+            part(1 - hi)
+            crossing()
+            part(hi)
 
     wd_done()
     branch_block(col_of[3], 1)
@@ -529,10 +565,9 @@
     X_qk = WN.at[:, pl.ds(0, hh)]
     V_qk, R_qk = WN.at[low, pl.ds(hh, hh)], WN.at[high, pl.ds(hh, hh)]
 
-    in_keep("up", 1, DUP, keep_u, S_up)
     pl.semaphore_wait(credit.at[0], 1)
-    cross("up1", S_up.at[1], wid, V_up)
-    crossed("dn1", R_dn)
+    in_keep("up", 1, DUP, keep_u, S_up, lambda: cross("up1", S_up.at[1], wid, V_up))
+    crossed("dn1", R_dn, both_tiles)
     in_give("up", 0, DUP, give_u, SLOPE.at[:, pl.ds(0, uh)], S_up)
     branch_block(col_of[2], 1)
     copies.start("ob2", OUTP.at[rows(col_of[2]), other], OZ2.at[:, other], {"col": col_of[2]})
@@ -593,9 +628,8 @@
     in_give("qk", 0, QKV, give_h, SLOPE.at[:, pl.ds(0, hh)], S_qk)
     pl.semaphore_wait(credit.at[1], 1)
     crossed("up1", R_up)
-    in_keep("qk", 1, QKV, keep_h, S_qk)
     pl.semaphore_wait(credit.at[2], 1)
-    cross("qk1", S_qk.at[1], wid, V_qk)
+    in_keep("qk", 1, QKV, keep_h, S_qk, lambda: cross("qk1", S_qk.at[1], wid, V_qk))
     in_keep("qk", 0, QKV, keep_h, S_qk)
     copies.start("qk0x", S_qk.at[0], X_qk, x_dev)
 
@@ -670,8 +704,8 @@
         return at(c * blk + i * sub, sub)
 
     def row_rest(buf, names, whole, landing, name):
-        for arrival in names:
-            copies.came(arrival)
+        for arrival, when in names:
+            copies.came(arrival, when)
 
         def part(i):
             rs = at(i * sub, sub)
@@ -692,8 +726,6 @@
             total = total + ref[rs, :].astype(F32)
         return total
 
-    at_end, between = lax.rem(c, 3) == 0, lax.rem(c, 3) != 0
-
     def x_block(s):
         b = col_of[s]
         copies.came(f"ey{s}")
@@ -723,9 +755,15 @@
 
         copies.start(f"eb{s}", N.at[rows(b), own], DZ.at[2], {"col": b}, between)
 
-    row_rest(OUTP, ("oa1", "oa2", "ob1", "ob2"), (OZ1, OZ2), OY.at[0], "oy0")
+    row_rest(
+        OUTP,
+        (("oa1", between), ("oc1", at_end), ("oa2", None), ("ob1", None), ("ob2", None)),
+        (OZ1, OZ2),
+        OY.at[0],
+        "oy0",
+    )
     spread_out("up1", R_up, g_up, up_at(1 - r, hi))
-    finish("dn0", S_dn.at[0], X_dn, g_down, down_at(r))
+    finish("dn0", S_dn.at[0], X_dn, g_down, down_at(r), both_tiles)
     finish("de0", S_de.at[0], X_de, g_dense, dense_at(r))
     finish("up0", S_up.at[0], X_up, g_up, up_at(r))
     crossed("qk1", R_qk)
@@ -738,7 +776,7 @@
     copies.start("eza", N.at[rows(col_of[1]), own], DZ1.at[:, own], {"col": col_of[1]})
     BS[...] = gathered_dp("b", BQ)
     copies.start("by", BS, BR, y_dev)
-    row_rest(N, ("ezb",), (DZ1,), EY[0], "ey0")
+    row_rest(N, (("ezb", None),), (DZ1,), EY[0], "ey0")
     x_pass(3)
     finish("qk0", S_qk.at[0], X_qk, g_qkv, qkv_at(r))
     pass_quarter("dn1", g_down, down_at(1 - r, 1 - hi))
@@ -758,11 +796,13 @@
         out[at(i * sub, sub), :] = (total + row_of(dense_b[...] + down_b[...])).astype(BF16)
 
     tiles(blk // sub, out_last)
+    fetch(out, out_hbm)
     pass_quarter("up1", g_up, up_at(1 - r, 1 - hi))
     copies.came("by")
     small[0:8, :] = BS[...]
     small[8:16, :] = BR[...]
     small[4:8, :] = gathered_dp("n", NQ)[0:4]
+    fetch(small, small_hbm)
     copies.came("eza")
     copies.came("eb2", at_end)
     copies.came("eb3", between)
@@ -773,6 +813,7 @@
         in_grad[at(i * sub, sub), :] = COT[at(i * sub, sub), :].astype(F32) + total
 
     tiles(blk // sub, x_last)
+    fetch(in_grad, in_grad_hbm)
     pass_quarter("qk1", g_qkv, qkv_at(1 - r, 1 - hi))
     for name in ("dn0", "de0", "up0", "qk0"):
         copies.came(f"{name}t")
@@ -792,7 +833,8 @@
     ]
     V = pltpu.VMEM
     return (
-        [V(shape, BF16) for shape in low]
+        [V((blk, wid), BF16), V((blk, wid), F32), V((16, wid), F32)]
+        + [V(shape, BF16) for shape in low]
         + [V((tokens, 128), F32)]
         + [
             V(shape, BF16)
@@ -889,7 +931,7 @@
             shape(down_weight.shape, BF16),
         ),
         in_specs=[far] * 6 + [vmem] * 9,
-        out_specs=(vmem,) * 3 + (far,) * 4,
+        out_specs=(far,) * 7,
         scratch_shapes=scratch(blk, wid, cols, units, heads),
         compiler_params=pltpu.CompilerParams(
             collective_id=0, has_side_effects=True, vmem_limit_bytes=67043328

time: 250 us -> 247 us (0.988)
  no operation moved by 1% of the time
where the time goes in v5:
time: 247 us; the launch traced here: 246 us
  Pallas kernels  245 us (99%)
    pallas_call x1, Pallas kernels, shards(): pl.pallas_call(functools.partial(step_kernel, (blk, wid, cols)), out_shap...  231 us
    pallas_call x1, Pallas kernels, shards(): pl.pallas_call(widen_kernel, grid=(steps,), out_shape=[shape(out.shape, B...  13.9 us

profile of v5, /device:TPU:9, one launch (start us, length us, event | category | flops | bytes accessed | tf_op | source)
XLA Modules:
  0.0 246.1 jit_solution(11533499049817738342)
XLA Ops:
  0.7 231.4 %step.1 = (bf16[256,1024]{1,0:T(8,128)(2,1)}, f32[256,1024]{1,0:T(8,128)}, f32[16,1024]{1,0:T(8,128)}, bf16[1024,1536]{1,0:T(8,128)(2,1)}, bf16[512,1024]{1,0:T(...) custom-call(bf16[256,1024]{1,0:T(8,128)(2,1)} %hid.1, bf16[256,1024]{1,0:T(8,128)(2,1)} %cot.1, ...), custom_call_target="tpu_custom_call" | custom-call | tf_op jit(solution)/shard_map/step/pallas_call | solution.py:922
  232.1 13.9 %widen.1 = (bf16[256,1024]{1,0:T(8,128)(2,1)}, f32[256,1024]{1,0:T(8,128)}, f32[1024,1536]{1,0:T(8,128)}, f32[512,1024]{1,0:T(8,128)}, f32[1024,2048]{1,0:T(8,12...) custom-call(bf16[256,1024]{1,0:T(8,128)(2,1)} %get-tuple-element.35., ...), custom_call_target="tpu_custom_call" | custom-call | tf_op jit(solution)/shard_map/widen/pallas_call | solution.py:962

commit v6 on v5

--- a/solution.py
+++ b/solution.py
@@ -80,7 +80,7 @@
     hid, cot, wq, wu, wd, wn, seg, gain1, bias1, gain2, bias2, qkv_b, up_b, dense_b, down_b,
     out_hbm, in_grad_hbm, small_hbm, g_qkv, g_dense, g_up, g_down,
     out, in_grad, small, X, G, WQ, WU, WD, WN, N, STAT, QKV, ATT, HID, SLOPE, DUP, DAT, OUTP, OZ1, OZ2, OZ3, OY, DZ1, DZ, COT,
-    S_dn, S_de, S_up, S_qk, R_dn, R_de, V_dn, V_de, X_dn, X_de, A_de, TMP, NV, COS, SIN, NSUM, SMO, SMR, NZ, NQ, BQ, BS, BR,
+    S_dn, S_de, S_up, S_qk, R_dn, R_de, V_dn, V_de, V_up, X_dn, X_de, A_de, TMP, NV, COS, SIN, NSUM, SMO, SMR, NZ, NQ, BQ, BS, BR,
     send_sem, recv_sem, local_sem, credit,
 ):
     blk, wid, cols = sizes
@@ -301,7 +301,9 @@
     norm_block(col_of[3])
     up_block(col_of[3])
     copies.came("gy")
-    chain_send("h", 1, G, other)
+    near_part, far_part = pl.ds(wid, wid // 2), pl.ds(wid + wid // 2, wid // 2)
+    chain_send("h", 1, G, near_part)
+    chain_send("i", 1, G, far_part)
 
     def grad_send(name, staged, left, right, n_rows, n_cols, target):
         def part(i):
@@ -339,16 +341,18 @@
 
     down_tiles = [slice(i * TILE, (i + 1) * TILE) for i in range(wid // TILE)]
 
-    def down_give(side, staged):
-        for i, cs in enumerate(down_tiles):
+    def down_give(side, staged, which):
+        for i in which:
+            cs = down_tiles[i]
             part = dot(HID[:, hid_send], G[:, side * wid + i * TILE : side * wid + (i + 1) * TILE], TN)
             staged[:, cs] = part.astype(BF16)
             copies.start(f"dn{side}a{i}", staged.at[:, cs], S_dn.at[side, :, cs], core_dev)
 
-    def down_keep(side):
+    def down_keep(side, which):
         half_rows = uh // 2
         give = at((1 - hi) * half_rows, half_rows)
-        for i, cs in enumerate(down_tiles):
+        for i in which:
+            cs = down_tiles[i]
             copies.came(f"dn{side}a{i}")
             mine = dot(HID[:, hid_keep], G[:, side * wid + i * TILE : side * wid + (i + 1) * TILE], TN)
             S_dn[side, :, cs] = (mine + S_dn[side, :, cs].astype(F32)).astype(BF16)
@@ -427,13 +431,27 @@
 
     chain_wait("g", 3)
     both_tiles = tuple(range(len(down_tiles)))
-    down_give(0, DUP.at[pl.ds(0, uh), :])
-    down_keep(0)
+    down_give(0, DUP.at[pl.ds(0, uh), :], both_tiles)
+    down_keep(0, both_tiles)
+    give_u, keep_u = at((1 - k) * uh, uh), at(k * uh, uh)
+
+    def hidden_back(i, side):
+        block = at(i * blk, blk)
+        TMP[:, at(i * uh, uh)] = dot(
+            G[block, side * wid : (side + 1) * wid], WN[give_u, side * wid : (side + 1) * wid], NT
+        )
+
 
     chain_wait("h", 1)
-    chain_send("h", 2, G, other)
+    chain_send("h", 2, G, near_part)
+    fetch_n.wait()
+    tiles(cols, lambda i: hidden_back(i, 0))
+    chain_wait("i", 1)
+    chain_send("i", 2, G, far_part)
     fetch_q.wait()
     wq_on()
+    chain_wait("h", 2)
+    chain_send("h", 3, G, near_part)
     wq_done()
 
     def qkv_block(i):
@@ -446,8 +464,8 @@
             QKV[block, j * HD : (j + 1) * HD] = value.astype(BF16)
 
     tiles(cols, qkv_block)
-    chain_wait("h", 2)
-    chain_send("h", 3, G, other)
+    chain_wait("i", 2)
+    chain_send("i", 3, G, far_part)
 
     def key_range(i):
         low = max(0, i - 2) * blk
@@ -472,7 +490,6 @@
         p_low = (p / total).astype(BF16)
         ATT[mine, :] = dot(p_low, QKV[span, 2 * HD :], NN).astype(BF16)
     out_grad("de0", 0, ATT, att_keep, att_send, A_de.at[0], S_de.at[0])
-    fetch_n.wait()
     fetch_d.wait()
 
     def branch_block(b, side):
@@ -486,10 +503,10 @@
     branch_block(col_of[2], 0)
     out_keep("de0", 0, ATT, att_keep, S_de.at[0])
     copies.start("de0x", S_de.at[0], X_de, x_dev)
-    for s in (3, 1, 0):
-        branch_block(col_of[s], 0)
+    branch_block(col_of[3], 0)
 
     chain_wait("h", 3)
+    down_give(1, DUP.at[pl.ds(uh, uh), :], both_tiles[:1])
     at_end, between = lax.rem(c, 3) == 0, lax.rem(c, 3) != 0
 
     def own_near(name, when):
@@ -497,30 +514,35 @@
             name, OUTP.at[rows(col_of[1]), own], OZ1.at[:, own], {"col": col_of[1]}, when
         )
 
+    for s in (1, 0):
+        branch_block(col_of[s], 0)
+    down_keep(1, both_tiles[:1])
+    chain_wait("i", 3)
     own_near("oa1", at_end)
-    down_give(1, DUP.at[pl.ds(uh, uh), :])
+    down_give(1, DUP.at[pl.ds(uh, uh), :], both_tiles[1:])
     out_grad("de1", 1, ATT, att_keep, att_send, A_de.at[1], S_de.at[1])
     wn_on()
-    down_keep(1)
+    down_keep(1, both_tiles[1:])
     halves["dn1"] = (S_dn.at[1, at(hi * (uh // 2), uh // 2), :], V_dn)
     out_keep("de1", 1, ATT, att_keep, S_de.at[1])
     cross("de1", S_de.at[1], dh, V_de)
     own_near("oc1", between)
     wn_done()
     copies.start("oa2", OUTP.at[rows(col_of[2]), own], OZ2.at[:, own], {"col": col_of[2]})
-    wd_on()
 
     copies.sent(*[f"dn{side}a{i}" for side in (0, 1) for i in both_tiles])
 
-    def up_grad_part(i):
+    def up_grad_give(i):
         block = at(i * blk, blk)
-        for j in range(units // TILE):
-            cs = slice(j * TILE, (j + 1) * TILE)
-            back = dot(G[block, :], WN[cs, :], NT)
-            DUP[block, cs] = (back * SLOPE[block, cs].astype(F32)).astype(BF16)
-
-    tiles(cols, up_grad_part)
-    keep_u, give_u = at(k * uh, uh), at((1 - k) * uh, uh)
+        back = TMP[:, at(i * uh, uh)] + dot(G[block, other], WN[give_u, other], NT)
+        DUP[block, give_u] = (back * SLOPE[block, give_u].astype(F32)).astype(BF16)
+
+    def up_grad_keep(i):
+        block = at(i * blk, blk)
+        back = dot(G[block, :], WN[keep_u, :], NT)
+        DUP[block, keep_u] = (back * SLOPE[block, keep_u].astype(F32)).astype(BF16)
+
+    tiles(cols, up_grad_give)
     keep_h, give_h = at(k * hh, hh), at((1 - k) * hh, hh)
 
     def in_give(name, side, right_ref, give, staged, landing):
@@ -548,30 +570,32 @@
             crossing()
             part(hi)
 
+    in_give("up", 1, DUP, give_u, SLOPE.at[:, give_u], S_up)
+    tiles(cols, up_grad_keep)
+    wd_on()
+    in_keep("up", 1, DUP, keep_u, S_up, lambda: cross("up1", S_up.at[1], wid, V_up))
     wd_done()
     branch_block(col_of[3], 1)
     copies.start("oy3", OUTP.at[rows(col_of[3]), other], OY.at[1], y_dev)
-    in_give("up", 1, DUP, give_u, SLOPE.at[:, pl.ds(uh, uh)], S_up)
     for i in range(cols):
         mine = slice(i * blk, (i + 1) * blk)
         DAT[mine, :] = dot(G[mine, :], WD[...], NT).astype(BF16)
     BQ[q, 2:3, :] = jnp.sum(G[:, own].astype(F32), axis=0, keepdims=True)
 
-    copies.sent(*[f"{t}{w}{s}" for t in "gh" for w in "ud" for s in (1, 2, 3)])
+    copies.sent(*[f"{t}{w}{s}" for t in "ghi" for w in "ud" for s in (1, 2, 3)])
     pl.semaphore_signal(credit.at[0], inc=1, device_id=x_dev, device_id_type=MESH)
     pl.semaphore_signal(credit.at[1], inc=1, device_id=y_dev, device_id_type=MESH)
-    X_up, low, high = G.at[:, pl.ds(0, uh)], pl.ds(0, wid // 2), pl.ds(wid // 2, wid // 2)
-    V_up, R_up = G.at[low, pl.ds(uh, uh)], G.at[high, pl.ds(uh, uh)]
+    low, high = pl.ds(0, wid // 2), pl.ds(wid // 2, wid // 2)
+    X_up, R_up = G.at[:, pl.ds(0, uh)], G.at[high, pl.ds(uh, uh)]
     X_qk = WN.at[:, pl.ds(0, hh)]
     V_qk, R_qk = WN.at[low, pl.ds(hh, hh)], WN.at[high, pl.ds(hh, hh)]
 
-    pl.semaphore_wait(credit.at[0], 1)
-    in_keep("up", 1, DUP, keep_u, S_up, lambda: cross("up1", S_up.at[1], wid, V_up))
+    in_give("up", 0, DUP, give_u, SLOPE.at[:, keep_u], S_up)
     crossed("dn1", R_dn, both_tiles)
-    in_give("up", 0, DUP, give_u, SLOPE.at[:, pl.ds(0, uh)], S_up)
     branch_block(col_of[2], 1)
     copies.start("ob2", OUTP.at[rows(col_of[2]), other], OZ2.at[:, other], {"col": col_of[2]})
     in_keep("up", 0, DUP, keep_u, S_up)
+    pl.semaphore_wait(credit.at[0], 1)
     copies.start("up0x", S_up.at[0], X_up, x_dev)
 
     branch_block(col_of[1], 1)
@@ -844,6 +868,7 @@
                 (2, blk, wid), (blk, width), (3, blk, wid), (blk, wid),
                 (2, units // 2, wid), (2, HD // 2, wid), (2, wid, units // 2), (2, wid, heads // 2),
                 (units // 4, wid), (HD // 4, wid), (units // 4, wid), (HD // 4, wid),
+                (wid // 2, units // 2),
                 (units // 2, wid), (HD // 2, wid), (2, HD // 2, wid),
             )
         ]

time: 247 us -> 242 us (0.980)
  Pallas kernels: 245 us -> 239 us
    pallas_call x1, Pallas kernels: 231 us -> 225 us  [shards(): pl.pallas_call(functools.partial(step_kernel, (blk, wid, cols)), out_shap...]
where the time goes in v6:
time: 242 us; the launch traced here: 240 us
  Pallas kernels  239 us (99%)
    pallas_call x1, Pallas kernels, shards(): pl.pallas_call(functools.partial(step_kernel, (blk, wid, cols)), out_shap...  225 us
    pallas_call x1, Pallas kernels, shards(): pl.pallas_call(widen_kernel, grid=(steps,), out_shape=[shape(out.shape, B...  13.9 us

profile of v6, /device:TPU:9, one launch (start us, length us, event | category | flops | bytes accessed | tf_op | source)
XLA Modules:
  0.0 240.1 jit_solution(9577280336686636116)
XLA Ops:
  0.7 225.4 %step.1 = (bf16[256,1024]{1,0:T(8,128)(2,1)}, f32[256,1024]{1,0:T(8,128)}, f32[16,1024]{1,0:T(8,128)}, bf16[1024,1536]{1,0:T(8,128)(2,1)}, bf16[512,1024]{1,0:T(...) custom-call(bf16[256,1024]{1,0:T(8,128)(2,1)} %hid.1, bf16[256,1024]{1,0:T(8,128)(2,1)} %cot.1, ...), custom_call_target="tpu_custom_call" | custom-call | tf_op jit(solution)/shard_map/step/pallas_call | solution.py:947
  226.0 13.9 %widen.1 = (bf16[256,1024]{1,0:T(8,128)(2,1)}, f32[256,1024]{1,0:T(8,128)}, f32[1024,1536]{1,0:T(8,128)}, f32[512,1024]{1,0:T(8,128)}, f32[1024,2048]{1,0:T(8,12...) custom-call(bf16[256,1024]{1,0:T(8,128)(2,1)} %get-tuple-element.35., ...), custom_call_target="tpu_custom_call" | custom-call | tf_op jit(solution)/shard_map/widen/pallas_call | solution.py:987

commit v7 on v6

--- a/solution.py
+++ b/solution.py
@@ -29,14 +29,20 @@
 class Copies:
     def __init__(self, send_sem, recv_sem):
         self.send_sem, self.recv_sem = send_sem, recv_sem
-        self.made, self.open = {}, {}
+        self.made, self.open, self.free, self.slot = {}, {}, [], {}
+        self.used = 0
 
     def start(self, name, source, target, device, when=None):
+        if self.free:
+            slot = self.free.pop(0)
+        else:
+            slot, self.used = self.used, self.used + 1
         index = len(self.made)
+        self.slot[name] = slot
         copy = pltpu.make_async_remote_copy(
             src_ref=source,
             dst_ref=target,
-            send_sem=self.send_sem.at[index],
+            send_sem=self.send_sem.at[slot],
             recv_sem=self.recv_sem.at[index],
             device_id=device,
             device_id_type=MESH,
@@ -51,6 +57,7 @@
     def sent(self, *names):
         for name in names:
             guarded(self.open.pop(name), self.made[name].wait_send)
+            self.free.append(self.slot[name])
 
     def sent_all(self):
         self.sent(*list(self.open))
@@ -78,9 +85,9 @@
 def step_kernel(
     sizes,
     hid, cot, wq, wu, wd, wn, seg, gain1, bias1, gain2, bias2, qkv_b, up_b, dense_b, down_b,
-    out_hbm, in_grad_hbm, small_hbm, g_qkv, g_dense, g_up, g_down,
-    out, in_grad, small, X, G, WQ, WU, WD, WN, N, STAT, QKV, ATT, HID, SLOPE, DUP, DAT, OUTP, OZ1, OZ2, OZ3, OY, DZ1, DZ, COT,
-    S_dn, S_de, S_up, S_qk, R_dn, R_de, V_dn, V_de, V_up, X_dn, X_de, A_de, TMP, NV, COS, SIN, NSUM, SMO, SMR, NZ, NQ, BQ, BS, BR,
+    out, in_grad, small, G, WN, WU, g_dense,
+    X, WQ, WD, N, STAT, QKV, ATT, HID, SLOPE, DUP, DAT, OUTP, OZ1, OZ2, OZ3, OY, DZ1, DZ,
+    S_dn, S_de, S_up, S_qk, R_dn, R_de, V_dn, V_de, V_up, X_dn, X_de, TMP, NV, COS, SIN, NSUM, SMO, SMR, NZ, NQ, BQ, BS, BR,
     send_sem, recv_sem, local_sem, credit,
 ):
     blk, wid, cols = sizes
@@ -123,7 +130,6 @@
         local.append(copy)
         return copy
 
-    fetch_c = fetch(cot, COT)
     fetch_x = fetch(hid, X.at[at(c * blk, blk), own])
     fetch_g = fetch(cot, G.at[at(c * blk, blk), own])
     fetch_u = fetch(wu.at[:, at(r * units, units)], WU.at[own, :])
@@ -253,7 +259,6 @@
 
         tiles(units // TILE, part)
 
-    fetch_c.wait()
     fetch_x.wait()
     fetch_g.wait()
     chain_wait("x", 1)
@@ -369,10 +374,16 @@
         copies.start(f"{name}x", total.at[give, :], landing, x_dev)
         halves[name] = (total.at[keep, :], landing)
 
-    def crossed(name, target, parts=("",)):
+    def down_crossed(i):
+        cs = down_tiles[i]
+        copies.came(f"dn1x{i}")
+        mine = S_dn[1, at(hi * (uh // 2), uh // 2), cs].astype(F32)
+        V_dn[:, cs] = (mine + V_dn[:, cs].astype(F32)).astype(BF16)
+        copies.start(f"dn1y{i}", V_dn.at[:, cs], R_dn.at[:, cs], y_dev)
+
+    def crossed(name, target):
         mine, landing = halves[name]
-        for word in parts:
-            copies.came(f"{name}x{word}")
+        copies.came(f"{name}x")
         n = landing.shape[0]
         step = min(n, 128)
 
@@ -383,29 +394,34 @@
         tiles(n // step, part)
         copies.start(f"{name}y", landing, target, y_dev)
 
-    def spread_out(name, came, result, here):
-        copies.came(f"{name}y")
-        copies.start(f"{name}g", came, result.at[here], x_dev)
-        copies.start(f"{name}t", came, result.at[here], core_dev)
-        fetch(came, result.at[here])
+    def spread_out(name, result, here, came=None, parts=("",)):
+        for word in parts:
+            copies.came(f"{name}y{word}")
+        source = result.at[here] if came is None else came
+        copies.start(f"{name}g", source, result.at[here], x_dev)
+        copies.start(f"{name}t", source, result.at[here], core_dev)
+        if came is not None:
+            fetch(came, result.at[here])
 
     def pass_quarter(name, result, there):
         copies.came(f"{name}g")
         copies.start(f"{name}f", result.at[there], result.at[there], core_dev)
 
-    def finish(name, total, came, result, here, parts=("",)):
+    def finish(name, total, result, here, came=None, parts=("",)):
         for word in parts:
             copies.came(f"{name}x{word}")
+        landed = result.at[here] if came is None else came
         n = total.shape[0]
         step = min(n, 128)
 
         def part(i):
             rs = at(i * step, step)
-            came[rs, :] = (total[rs, :].astype(F32) + came[rs, :].astype(F32)).astype(BF16)
+            landed[rs, :] = (total[rs, :].astype(F32) + landed[rs, :].astype(F32)).astype(BF16)
 
         tiles(n // step, part)
-        copies.start(f"{name}t", came, result.at[here], core_dev)
-        fetch(came, result.at[here])
+        copies.start(f"{name}t", landed, result.at[here], core_dev)
+        if came is not None:
+            fetch(came, result.at[here])
 
     wide = slice(None)
 
@@ -450,8 +466,6 @@
     chain_send("i", 2, G, far_part)
     fetch_q.wait()
     wq_on()
-    chain_wait("h", 2)
-    chain_send("h", 3, G, near_part)
     wq_done()
 
     def qkv_block(i):
@@ -464,8 +478,8 @@
             QKV[block, j * HD : (j + 1) * HD] = value.astype(BF16)
 
     tiles(cols, qkv_block)
-    chain_wait("i", 2)
-    chain_send("i", 3, G, far_part)
+    chain_wait("h", 2)
+    chain_send("h", 3, G, near_part)
 
     def key_range(i):
         low = max(0, i - 2) * blk
@@ -489,7 +503,10 @@
         STAT[mine, 2:3] = largest + jnp.log(total)
         p_low = (p / total).astype(BF16)
         ATT[mine, :] = dot(p_low, QKV[span, 2 * HD :], NN).astype(BF16)
-    out_grad("de0", 0, ATT, att_keep, att_send, A_de.at[0], S_de.at[0])
+    copies.sent("dn0a0", "dn0a1")
+    out_grad("de0", 0, ATT, att_keep, att_send, DUP.at[pl.ds(0, dh), :], S_de.at[0])
+    chain_wait("i", 2)
+    chain_send("i", 3, G, far_part)
     fetch_d.wait()
 
     def branch_block(b, side):
@@ -520,17 +537,16 @@
     chain_wait("i", 3)
     own_near("oa1", at_end)
     down_give(1, DUP.at[pl.ds(uh, uh), :], both_tiles[1:])
-    out_grad("de1", 1, ATT, att_keep, att_send, A_de.at[1], S_de.at[1])
-    wn_on()
+    out_grad("de1", 1, ATT, att_keep, att_send, DUP.at[pl.ds(dh, dh), :], S_de.at[1])
     down_keep(1, both_tiles[1:])
-    halves["dn1"] = (S_dn.at[1, at(hi * (uh // 2), uh // 2), :], V_dn)
     out_keep("de1", 1, ATT, att_keep, S_de.at[1])
     cross("de1", S_de.at[1], dh, V_de)
+    wn_on()
     own_near("oc1", between)
     wn_done()
     copies.start("oa2", OUTP.at[rows(col_of[2]), own], OZ2.at[:, own], {"col": col_of[2]})
 
-    copies.sent(*[f"dn{side}a{i}" for side in (0, 1) for i in both_tiles])
+    copies.sent("dn1a0", "dn1a1", "de0a", "de1a")
 
     def up_grad_give(i):
         block = at(i * blk, blk)
@@ -543,6 +559,7 @@
         DUP[block, keep_u] = (back * SLOPE[block, keep_u].astype(F32)).astype(BF16)
 
     tiles(cols, up_grad_give)
+    down_crossed(0)
     keep_h, give_h = at(k * hh, hh), at((1 - k) * hh, hh)
 
     def in_give(name, side, right_ref, give, staged, landing):
@@ -582,21 +599,21 @@
         DAT[mine, :] = dot(G[mine, :], WD[...], NT).astype(BF16)
     BQ[q, 2:3, :] = jnp.sum(G[:, own].astype(F32), axis=0, keepdims=True)
 
-    copies.sent(*[f"{t}{w}{s}" for t in "ghi" for w in "ud" for s in (1, 2, 3)])
+    copies.sent(*[f"{t}{w}{s}" for t in "xghi" for w in "ud" for s in (1, 2, 3)])
+    copies.sent("xy0", "xy1", "xy2", "xy3", "gy", "nv", "wuy", "wux", "wuc", "wuf", "wqy", "wqc")
+    copies.sent("dn0x0", "dn0x1", "wny", "wdy", "wdc")
     pl.semaphore_signal(credit.at[0], inc=1, device_id=x_dev, device_id_type=MESH)
     pl.semaphore_signal(credit.at[1], inc=1, device_id=y_dev, device_id_type=MESH)
-    low, high = pl.ds(0, wid // 2), pl.ds(wid // 2, wid // 2)
-    X_up, R_up = G.at[:, pl.ds(0, uh)], G.at[high, pl.ds(uh, uh)]
-    X_qk = WN.at[:, pl.ds(0, hh)]
-    V_qk, R_qk = WN.at[low, pl.ds(hh, hh)], WN.at[high, pl.ds(hh, hh)]
+    pl.semaphore_signal(credit.at[5], inc=1, device_id=core_dev, device_id_type=MESH)
+    V_qk = WN.at[pl.ds(0, wid // 2), pl.ds(2 * heads, hh)]
 
     in_give("up", 0, DUP, give_u, SLOPE.at[:, keep_u], S_up)
-    crossed("dn1", R_dn, both_tiles)
+    down_crossed(1)
     branch_block(col_of[2], 1)
     copies.start("ob2", OUTP.at[rows(col_of[2]), other], OZ2.at[:, other], {"col": col_of[2]})
     in_keep("up", 0, DUP, keep_u, S_up)
     pl.semaphore_wait(credit.at[0], 1)
-    copies.start("up0x", S_up.at[0], X_up, x_dev)
+    copies.start("up0x", S_up.at[0], G.at[up_at(r)], x_dev)
 
     branch_block(col_of[1], 1)
     copies.start("ob1", OUTP.at[rows(col_of[1]), other], OZ1.at[:, other], {"col": col_of[1]})
@@ -605,6 +622,7 @@
     copies.sent("wnc")
     pl.semaphore_signal(credit.at[2], inc=1, device_id=x_dev, device_id_type=MESH)
     pl.semaphore_signal(credit.at[3], inc=1, device_id=y_dev, device_id_type=MESH)
+    pl.semaphore_signal(credit.at[6], inc=1, device_id=core_dev, device_id_type=MESH)
     pl.semaphore_signal(credit.at[4], inc=1, device_id=y_dev, device_id_type=MESH)
 
     def out_block():
@@ -651,11 +669,11 @@
     in_give("qk", 1, QKV, give_h, SLOPE.at[:, pl.ds(hh, hh)], S_qk)
     in_give("qk", 0, QKV, give_h, SLOPE.at[:, pl.ds(0, hh)], S_qk)
     pl.semaphore_wait(credit.at[1], 1)
-    crossed("up1", R_up)
+    crossed("up1", G.at[up_at(r, hi)])
     pl.semaphore_wait(credit.at[2], 1)
     in_keep("qk", 1, QKV, keep_h, S_qk, lambda: cross("qk1", S_qk.at[1], wid, V_qk))
     in_keep("qk", 0, QKV, keep_h, S_qk)
-    copies.start("qk0x", S_qk.at[0], X_qk, x_dev)
+    copies.start("qk0x", S_qk.at[0], WN.at[qkv_at(r)], x_dev)
 
     def gather_dp(name, slots):
         for word, device in (("c", core_dev), ("x", x_dev), ("d", far_dev)):
@@ -713,14 +731,15 @@
         copies.start(f"ey{s}", N.at[rows(col_of[s]), other], EY[s - 1], y_dev)
         if s == 2:
             out_block()
-            spread_out("dn1", R_dn, g_down, down_at(1 - r, hi))
         else:
-            spread_out("de1", R_de, g_dense, dense_at(1 - r, hi))
+            spread_out("de1", g_dense, dense_at(1 - r, hi), R_de)
     norm_back(col_of[1])
     copies.start(
         "ezb", N.at[rows(col_of[1]), other], DZ1.at[:, other], {"col": col_of[1]}
     )
     norm_back(col_of[0])
+    pl.semaphore_signal(credit.at[7], inc=1, device_id=core_dev, device_id_type=MESH)
+    pl.semaphore_signal(credit.at[8], inc=1, device_id=x_dev, device_id_type=MESH)
     SMO[0:4, :] = NSUM[0:4, other]
     copies.start("sy", SMO, SMR, y_dev)
 
@@ -786,11 +805,15 @@
         OY.at[0],
         "oy0",
     )
-    spread_out("up1", R_up, g_up, up_at(1 - r, hi))
-    finish("dn0", S_dn.at[0], X_dn, g_down, down_at(r), both_tiles)
-    finish("de0", S_de.at[0], X_de, g_dense, dense_at(r))
-    finish("up0", S_up.at[0], X_up, g_up, up_at(r))
-    crossed("qk1", R_qk)
+    pl.semaphore_wait(credit.at[7], 1)
+    pl.semaphore_wait(credit.at[8], 1)
+    spread_out("dn1", WU, down_at(1 - r, hi), R_dn, both_tiles)
+    pl.semaphore_wait(credit.at[5], 1)
+    spread_out("up1", G, up_at(1 - r, hi))
+    finish("dn0", S_dn.at[0], WU, down_at(r), X_dn, both_tiles)
+    finish("de0", S_de.at[0], g_dense, dense_at(r), X_de)
+    finish("up0", S_up.at[0], G, up_at(r))
+    crossed("qk1", WN.at[qkv_at(r, hi)])
     x_block(2)
     copies.came("sy")
     NZ[c, 0:4, :] = NSUM[0:4, own] + SMR[0:4, :]
@@ -802,15 +825,16 @@
     copies.start("by", BS, BR, y_dev)
     row_rest(N, (("ezb", None),), (DZ1,), EY[0], "ey0")
     x_pass(3)
-    finish("qk0", S_qk.at[0], X_qk, g_qkv, qkv_at(r))
-    pass_quarter("dn1", g_down, down_at(1 - r, 1 - hi))
+    pl.semaphore_wait(credit.at[6], 1)
+    finish("qk0", S_qk.at[0], WN, qkv_at(r))
+    pass_quarter("dn1", WU, down_at(1 - r, 1 - hi))
     x_pass(2)
     for s in (1, 2, 3):
         copies.came(f"sz{s}")
     NQ[q] = NZ[0] + NZ[1] + NZ[2] + NZ[3]
     gather_dp("n", NQ)
     pass_quarter("de1", g_dense, dense_at(1 - r, 1 - hi))
-    spread_out("qk1", R_qk, g_qkv, qkv_at(1 - r, hi))
+    spread_out("qk1", WN, qkv_at(1 - r, hi))
     for name in ("oz3", "oy0"):
         copies.came(name)
 
@@ -820,56 +844,54 @@
         out[at(i * sub, sub), :] = (total + row_of(dense_b[...] + down_b[...])).astype(BF16)
 
     tiles(blk // sub, out_last)
-    fetch(out, out_hbm)
-    pass_quarter("up1", g_up, up_at(1 - r, 1 - hi))
+    again_g = X.at[pl.ds(0, blk), own]
+    fetch_c = pltpu.make_async_copy(cot, again_g, local_sem.at[11])
+    fetch_c.start()
+    pass_quarter("up1", G, up_at(1 - r, 1 - hi))
     copies.came("by")
     small[0:8, :] = BS[...]
     small[8:16, :] = BR[...]
     small[4:8, :] = gathered_dp("n", NQ)[0:4]
-    fetch(small, small_hbm)
     copies.came("eza")
     copies.came("eb2", at_end)
     copies.came("eb3", between)
     copies.came("ey0")
 
+    fetch_c.wait()
+
     def x_last(i):
         total = total_of(i, N, (DZ1,), (DZ.at[2], EY[0]))
-        in_grad[at(i * sub, sub), :] = COT[at(i * sub, sub), :].astype(F32) + total
+        in_grad[at(i * sub, sub), :] = again_g[at(i * sub, sub), :].astype(F32) + total
 
     tiles(blk // sub, x_last)
-    fetch(in_grad, in_grad_hbm)
-    pass_quarter("qk1", g_qkv, qkv_at(1 - r, 1 - hi))
+    pass_quarter("qk1", WN, qkv_at(1 - r, 1 - hi))
     for name in ("dn0", "de0", "up0", "qk0"):
         copies.came(f"{name}t")
     for name in ("dn1", "de1", "up1", "qk1"):
         copies.came(f"{name}t")
         copies.came(f"{name}f")
-    for copy in local[7:]:
+    for copy in local[6:]:
         copy.wait()
     copies.sent_all()
 
 
 def scratch(blk, wid, cols, units, heads):
     tokens, width = blk * cols, 2 * wid
-    low = [
-        (tokens, width), (tokens, width), (width, heads), (width, units), (HD, width),
-        (units, width), (tokens, width),
-    ]
+    low = [(tokens, width), (width, heads), (HD, width), (tokens, width)]
     V = pltpu.VMEM
     return (
-        [V((blk, wid), BF16), V((blk, wid), F32), V((16, wid), F32)]
-        + [V(shape, BF16) for shape in low]
+        [V(shape, BF16) for shape in low]
         + [V((tokens, 128), F32)]
         + [
             V(shape, BF16)
             for shape in (
                 (tokens, heads), (tokens, HD), (tokens, units), (tokens, units), (tokens, units),
                 (tokens, HD), (tokens, width), (blk, width), (blk, width), (blk, wid),
-                (2, blk, wid), (blk, width), (3, blk, wid), (blk, wid),
+                (2, blk, wid), (blk, width), (3, blk, wid),
                 (2, units // 2, wid), (2, HD // 2, wid), (2, wid, units // 2), (2, wid, heads // 2),
                 (units // 4, wid), (HD // 4, wid), (units // 4, wid), (HD // 4, wid),
                 (wid // 2, units // 2),
-                (units // 2, wid), (HD // 2, wid), (2, HD // 2, wid),
+                (units // 2, wid), (HD // 2, wid),
             )
         ]
         + [
@@ -885,32 +907,68 @@
             V((4, 8, wid), F32),
             V((8, wid), F32),
             V((8, wid), F32),
-            pltpu.SemaphoreType.DMA((120,)),
-            pltpu.SemaphoreType.DMA((120,)),
-            pltpu.SemaphoreType.DMA((20,)),
-            pltpu.SemaphoreType.REGULAR((5,)),
+            pltpu.SemaphoreType.DMA((60,)),
+            pltpu.SemaphoreType.DMA((110,)),
+            pltpu.SemaphoreType.DMA((12,)),
+            pltpu.SemaphoreType.REGULAR((9,)),
         ]
     )
 
 
-def widen_kernel(*refs):
-    given, results = refs[:7], refs[7:]
-    small = given[6]
-    for source, target in zip(given[:6], results[:6]):
-        target[...] = source[...].astype(target.dtype)
-
-    @pl.when(pl.program_id(0) == 0)
-    def _():
-        gain1, bias1, gain2, bias2, qkv_sum, dense_sum, up_sum, down_sum = results[6:]
-        for j, ref in enumerate((gain1, bias1, gain2, bias2)):
-            ref[...] = small[4 + j]
-        dense_sum[...] = small[2]
-        down_sum[...] = small[2]
-        r = lax.axis_index("row")
-        for ref, index in ((up_sum, 0), (qkv_sum, 1)):
-            n = ref.shape[0] // 2
-            ref[at(r * n, n)] = small[index, 0:n]
-            ref[at((1 - r) * n, n)] = small[8 + index, 0:n]
+WIDEN_DEPTH, WIDEN_ROWS, WIDEN_COLS = 4, 512, 1024
+
+
+def widen_kernel(
+    out, in_grad, small, g_up, g_qkv, g_down, g_dense,
+    out_hbm, in_grad_hbm, d_qkv, d_dense, d_up, d_down, *rest,
+):
+    sums_hbm, (buf, dense, sem, small_sem), sums = rest[:8], rest[8:12], rest[12:]
+    fetch = pltpu.make_async_copy(g_dense, dense, small_sem.at[0])
+    fetch.start()
+    jobs = []
+    for source, target in ((g_up, d_up), (g_down, d_down), (g_qkv, d_qkv), (dense, d_dense)):
+        n_rows, n_cols = target.shape
+        for row in range(0, n_rows, WIDEN_ROWS):
+            for col in range(0, n_cols, WIDEN_COLS):
+                span = min(WIDEN_COLS, n_cols - col)
+                jobs.append((source, target, row, col, span))
+    sent = []
+    for j, (source, target, row, col, span) in enumerate(jobs):
+        slot = j % WIDEN_DEPTH
+        if j >= WIDEN_DEPTH:
+            sent[j - WIDEN_DEPTH].wait()
+        if source is dense:
+            fetch.wait()
+        for part in range(0, WIDEN_ROWS, 64):
+            buf[slot, part : part + 64, 0:span] = source[
+                row + part : row + part + 64, col : col + span
+            ].astype(F32)
+        copy = pltpu.make_async_copy(
+            buf.at[slot, :, pl.ds(0, span)],
+            target.at[pl.ds(row, WIDEN_ROWS), pl.ds(col, span)],
+            sem.at[slot],
+        )
+        copy.start()
+        sent.append(copy)
+        if j == 1:
+            gain1, bias1, gain2, bias2, qkv_sum, dense_sum, up_sum, down_sum = sums
+            for i, ref in enumerate((gain1, bias1, gain2, bias2)):
+                ref[...] = small[4 + i]
+            dense_sum[...] = small[2]
+            down_sum[...] = small[2]
+            r = lax.axis_index("row")
+            for ref, index in ((up_sum, 0), (qkv_sum, 1)):
+                n = ref.shape[0] // 2
+                ref[at(r * n, n)] = small[index, 0:n]
+                ref[at((1 - r) * n, n)] = small[8 + index, 0:n]
+            pairs = [(out, out_hbm), (in_grad, in_grad_hbm), *zip(sums, sums_hbm)]
+            plain = [
+                pltpu.make_async_copy(a, b, small_sem.at[1 + i]) for i, (a, b) in enumerate(pairs)
+            ]
+            for copy in plain:
+                copy.start()
+    for copy in sent[-WIDEN_DEPTH:] + plain:
+        copy.wait()
 
 
 def swap(value, axis, mask):
@@ -944,29 +1002,31 @@
     vmem = pl.BlockSpec(memory_space=pltpu.VMEM)
     far = pl.BlockSpec(memory_space=pl.ANY)
     shape = jax.ShapeDtypeStruct
-    out, in_grad, small, g_qkv, g_dense, g_up, g_down = pl.pallas_call(
+    V = pltpu.VMEM
+    width, units_all, heads_all = 2 * wid, 2 * units, 2 * heads
+    out, in_grad, small, g_up, g_qkv, g_down, g_dense = pl.pallas_call(
         functools.partial(step_kernel, (blk, wid, cols)),
         out_shape=(
-            shape((blk, wid), BF16),
-            shape((blk, wid), F32),
-            shape((16, wid), F32),
-            shape(qkv_weight.shape, BF16),
+            V((blk, wid), BF16),
+            V((blk, wid), F32),
+            V((16, wid), F32),
+            V((blk * cols, width), BF16),
+            V((units, width), BF16),
+            V((width, units), BF16),
             shape(dense_weight.shape, BF16),
-            shape(up_weight.shape, BF16),
-            shape(down_weight.shape, BF16),
         ),
         in_specs=[far] * 6 + [vmem] * 9,
-        out_specs=(far,) * 7,
+        out_specs=(vmem,) * 6 + (far,),
         scratch_shapes=scratch(blk, wid, cols, units, heads),
         compiler_params=pltpu.CompilerParams(
-            collective_id=0, has_side_effects=True, vmem_limit_bytes=67043328
+            collective_id=0, has_side_effects=True, vmem_limit_bytes=52743168
         ),
         name="step",
     )(
         hidden_in, cotangent, qkv_weight, up_weight, dense_weight, down_weight, segment, *vectors
     )
 
-    grads = (g_qkv, g_dense, g_up, g_down)
+    grads = (g_up, g_qkv, g_down, g_dense)
     mask = 4
     while mask < lax.axis_size("dp"):
         grads = tuple(
@@ -974,29 +1034,30 @@
         )
         small = small + swap(small, "dp", mask)
         mask *= 2
-    steps = 4
-
-    def cut(array):
-        rows, columns = array.shape
-        return pl.BlockSpec((rows // steps, columns), lambda i: (i, 0))
-
-    def whole(n):
-        return pl.BlockSpec((n,), lambda i: (0,))
-
-    lengths = [wid] * 4 + [2 * heads, wid, 2 * units, wid]
+    lengths = [wid] * 4 + [heads_all, wid, units_all, wid]
+    results = [
+        (out.shape, BF16),
+        (in_grad.shape, F32),
+        (qkv_weight.shape, F32),
+        (dense_weight.shape, F32),
+        (up_weight.shape, F32),
+        (down_weight.shape, F32),
+    ]
     widened = pl.pallas_call(
         widen_kernel,
-        grid=(steps,),
-        out_shape=[shape(out.shape, BF16), shape(in_grad.shape, F32)]
-        + [shape(g.shape, F32) for g in grads]
-        + [shape((n,), F32) for n in lengths],
-        in_specs=[cut(out), cut(in_grad)]
-        + [cut(g) for g in grads]
-        + [pl.BlockSpec(small.shape, lambda i: (0, 0))],
-        out_specs=[cut(out), cut(in_grad)] + [cut(g) for g in grads] + [whole(n) for n in lengths],
-        compiler_params=pltpu.CompilerParams(vmem_limit_bytes=60 << 20),
+        out_shape=[shape(*result) for result in results] + [shape((n,), F32) for n in lengths],
+        in_specs=[vmem] * 6 + [pl.BlockSpec(memory_space=pltpu.HBM)],
+        out_specs=[far] * (len(results) + len(lengths)),
+        scratch_shapes=[
+            V((WIDEN_DEPTH, WIDEN_ROWS, WIDEN_COLS), F32),
+            V(dense_weight.shape, BF16),
+            pltpu.SemaphoreType.DMA((WIDEN_DEPTH,)),
+            pltpu.SemaphoreType.DMA((3 + len(lengths),)),
+        ]
+        + [V((n,), F32) for n in lengths],
+        compiler_params=pltpu.CompilerParams(vmem_limit_bytes=12 << 20),
         name="widen",
-    )(out, in_grad, *grads, small)
+    )(out, in_grad, small, *grads)
     out, in_grad, d_qkv, d_dense, d_up, d_down, *sums = widened
     return (
         out,

time: 242 us -> 237 us (0.979)
  Pallas kernels: 239 us -> 233 us
    pallas_call x1, Pallas kernels: 13.9 us -> 9.14 us  [shards(): pl.pallas_call(widen_kernel, out_shape=[shape(*result) for result in resu...]
where the time goes in v7:
time: 237 us; the launch traced here: 235 us
  Pallas kernels  233 us (98%)
    pallas_call x1, Pallas kernels, shards(): pl.pallas_call(functools.partial(step_kernel, (blk, wid, cols)), out_shap...  224 us
    pallas_call x1, Pallas kernels, shards(): pl.pallas_call(widen_kernel, out_shape=[shape(*result) for result in resu...  9.14 us

profile of v7, /device:TPU:9, one launch (start us, length us, event | category | flops | bytes accessed | tf_op | source)
XLA Modules:
  0.0 235.5 jit_solution(132882346968537702)
XLA Ops:
  0.7 224.3 %step.1 = (bf16[256,1024]{1,0:T(8,128)(2,1)S(1)}, f32[256,1024]{1,0:T(8,128)S(1)}, f32[16,1024]{1,0:T(8,128)S(1)}, bf16[1024,2048]{1,0:T(8,128)(2,1)S(1)}, bf16[...) custom-call(bf16[256,1024]{1,0:T(8,128)(2,1)} %hid.1, bf16[256,1024]{1,0:T(8,128)(2,1)} %cot.1, ...), custom_call_target="tpu_custom_call" | custom-call | tf_op jit(solution)/shard_map/step/pallas_call | solution.py:1007
  225.0 0.0 copy-start
  225.0 1.2 copy-done
  226.2 9.1 %widen.1 = (bf16[256,1024]{1,0:T(8,128)(2,1)}, f32[256,1024]{1,0:T(8,128)}, f32[1024,1536]{1,0:T(8,128)}, f32[512,1024]{1,0:T(8,128)}, f32[1024,2048]{1,0:T(8,12...) custom-call(bf16[256,1024]{1,0:T(8,128)(2,1)S(1)} %get-tuple-element, ...), custom_call_target="tpu_custom_call" | custom-call | tf_op jit(solution)/shard_map/widen/pallas_call | solution.py:1046
Async XLA Ops:
  225.0 1.2 copy-start

commit v8 on v7

--- a/solution.py
+++ b/solution.py
@@ -919,14 +919,12 @@
 
 
 def widen_kernel(
-    out, in_grad, small, g_up, g_qkv, g_down, g_dense,
-    out_hbm, in_grad_hbm, d_qkv, d_dense, d_up, d_down, *rest,
+    out, in_grad, small, g_up, g_qkv, g_down,
+    out_hbm, in_grad_hbm, d_qkv, d_up, d_down, *rest,
 ):
-    sums_hbm, (buf, dense, sem, small_sem), sums = rest[:8], rest[8:12], rest[12:]
-    fetch = pltpu.make_async_copy(g_dense, dense, small_sem.at[0])
-    fetch.start()
+    sums_hbm, (buf, sem, small_sem), sums = rest[:8], rest[8:11], rest[11:]
     jobs = []
-    for source, target in ((g_up, d_up), (g_down, d_down), (g_qkv, d_qkv), (dense, d_dense)):
+    for source, target in ((g_up, d_up), (g_down, d_down), (g_qkv, d_qkv)):
         n_rows, n_cols = target.shape
         for row in range(0, n_rows, WIDEN_ROWS):
             for col in range(0, n_cols, WIDEN_COLS):
@@ -937,8 +935,6 @@
         slot = j % WIDEN_DEPTH
         if j >= WIDEN_DEPTH:
             sent[j - WIDEN_DEPTH].wait()
-        if source is dense:
-            fetch.wait()
         for part in range(0, WIDEN_ROWS, 64):
             buf[slot, part : part + 64, 0:span] = source[
                 row + part : row + part + 64, col : col + span
@@ -963,7 +959,7 @@
                 ref[at((1 - r) * n, n)] = small[8 + index, 0:n]
             pairs = [(out, out_hbm), (in_grad, in_grad_hbm), *zip(sums, sums_hbm)]
             plain = [
-                pltpu.make_async_copy(a, b, small_sem.at[1 + i]) for i, (a, b) in enumerate(pairs)
+                pltpu.make_async_copy(a, b, small_sem.at[i]) for i, (a, b) in enumerate(pairs)
             ]
             for copy in plain:
                 copy.start()
@@ -1039,26 +1035,25 @@
         (out.shape, BF16),
         (in_grad.shape, F32),
         (qkv_weight.shape, F32),
-        (dense_weight.shape, F32),
         (up_weight.shape, F32),
         (down_weight.shape, F32),
     ]
     widened = pl.pallas_call(
         widen_kernel,
         out_shape=[shape(*result) for result in results] + [shape((n,), F32) for n in lengths],
-        in_specs=[vmem] * 6 + [pl.BlockSpec(memory_space=pltpu.HBM)],
+        in_specs=[vmem] * 6,
         out_specs=[far] * (len(results) + len(lengths)),
         scratch_shapes=[
             V((WIDEN_DEPTH, WIDEN_ROWS, WIDEN_COLS), F32),
-            V(dense_weight.shape, BF16),
             pltpu.SemaphoreType.DMA((WIDEN_DEPTH,)),
-            pltpu.SemaphoreType.DMA((3 + len(lengths),)),
+            pltpu.SemaphoreType.DMA((2 + len(lengths),)),
         ]
         + [V((n,), F32) for n in lengths],
         compiler_params=pltpu.CompilerParams(vmem_limit_bytes=12 << 20),
         name="widen",
-    )(out, in_grad, small, *grads)
-    out, in_grad, d_qkv, d_dense, d_up, d_down, *sums = widened
+    )(out, in_grad, small, *grads[:3])
+    d_dense = grads[3].astype(F32)
+    out, in_grad, d_qkv, d_up, d_down, *sums = widened
     return (
         out,
         in_grad,

time: 237 us -> 236 us (level)
  no operation moved by 1% of the time
where the time goes in v8:
time: 236 us; the launch traced here: 235 us
  Pallas kernels  233 us (99%)
    pallas_call x1, Pallas kernels, shards(): pl.pallas_call(functools.partial(step_kernel, (blk, wid, cols)), out_shap...  224 us
    pallas_call x1, Pallas kernels, shards(): pl.pallas_call(widen_kernel, out_shape=[shape(*result) for result in resu...  8.41 us

profile of v8, /device:TPU:9, one launch (start us, length us, event | category | flops | bytes accessed | tf_op | source)
XLA Modules:
  0.0 235.0 jit_solution(15113544976923781597)
XLA Ops:
  0.7 224.3 %step.1 = (bf16[256,1024]{1,0:T(8,128)(2,1)S(1)}, f32[256,1024]{1,0:T(8,128)S(1)}, f32[16,1024]{1,0:T(8,128)S(1)}, bf16[1024,2048]{1,0:T(8,128)(2,1)S(1)}, bf16[...) custom-call(bf16[256,1024]{1,0:T(8,128)(2,1)} %hid.1, bf16[256,1024]{1,0:T(8,128)(2,1)} %cot.1, ...), custom_call_target="tpu_custom_call" | custom-call | tf_op jit(solution)/shard_map/step/pallas_call | solution.py:1003
  225.0 0.0 copy-start
  225.0 8.4 %widen.1 = (bf16[256,1024]{1,0:T(8,128)(2,1)}, f32[256,1024]{1,0:T(8,128)}, f32[1024,1536]{1,0:T(8,128)}, f32[1024,2048]{1,0:T(8,128)}, f32[2048,1024]{1,0:T(8,1...) custom-call(bf16[256,1024]{1,0:T(8,128)(2,1)S(1)} %get-tuple-element, ...), custom_call_target="tpu_custom_call" | custom-call | tf_op jit(solution)/shard_map/widen/pallas_call | solution.py:1041
  233.4 0.0 copy-done
  233.4 1.6 convert_element_type.3
Async XLA Ops:
  225.0 8.4 %copy-start = (bf16[512,1024]{1,0:T(8,128)(2,1)S(1)}, bf16[512,1024]{1,0:T(8,128)(2,1)}, u32[]{:S(2)}) copy-start(bf16[512,1024]{1,0:T(8,128)(2,1)} %get-tuple-element.48) | copy-start | bytes 3145732
